TPU v7x, 32 devices: a whole 2x2x4 slice. The times are simulated.
32 devices in a mesh: wide: 8 (over z, x), grp: 4 (over y, core).
Axes of the slice: x: 2, y: 2, z: 4, core: 2. Of those that a mesh axis runs over, the one named last changes fastest.
Arguments:
- rows_in: bfloat16 [4096, 7168], P('wide', 'grp'), may hold values from -6 to 6
- upstream: bfloat16 [4096, 7168], P('wide', 'grp'), may hold values from -1.5 to 1.5
- probs: float32 [4096], P('wide'), may hold values from 0.05 to 1
- route: int32 [4096, 1], P('wide'), may hold values from 0 to 7; in each aligned block of 512 rows (0 to 511, 512 to 1023, ...) at most 96 rows name the same one
- live: int32 [8], P('wide'), may hold values from 96 to 512, as said below
- gate_up: bfloat16 [8, 7168, 2048], P('wide', 'grp'), may hold values from -0.0625 to 0.0625
- down: bfloat16 [8, 1024, 7168], P('wide', None, 'grp'), may hold values from -0.1875 to 0.1875
Outputs:
- grad_rows: bfloat16 [4096, 7168], P('wide', 'grp')
- grad_prob: bfloat16 [4096], P('wide')
- grad_gate_up: bfloat16 [8, 7168, 2048], P('wide', 'grp')
- grad_down: bfloat16 [8, 1024, 7168], P('wide', None, 'grp')
Inputs may be any that keep to these rules, and one draw needn't show every extreme that they name: `route`: in each aligned block of 512 rows no expert is named by more than 96 rows, a bound that some block reaches; every expert is named somewhere. Some block is live in full.
All inputs are finite; a program needn't handle non-finite values.
Results may differ from a plain program's by a relative error of at most 0.01.
Values may be sent and summed in bfloat16 or wider, within the bound.
No kernel may reach another device: no remote copies, remote signals or barrier semaphores. Data moves between devices by JAX's collectives and lax.ppermute only.
A program may use at most 128 MiB of HBM per device.

v0:
```python
import jax
import jax.numpy as jnp
from jax import lax
from jax.sharding import PartitionSpec as P

BALANCE = 1.0


def activate(gate, up, grad_hidden):
    sigmoid_gate = jax.nn.sigmoid(gate)
    swish = gate * sigmoid_gate
    hidden = (swish * up).astype(jnp.bfloat16)
    grad_gate = (grad_hidden * up * sigmoid_gate * (1.0 + gate * (1.0 - sigmoid_gate))).astype(
        jnp.bfloat16
    )
    grad_up = (grad_hidden * swish).astype(jnp.bfloat16)
    return (hidden, grad_gate, grad_up)


def contract_rows(left, right):
    return lax.dot_general(
        left, right, (((0,), (0,)), ((), ())), preferred_element_type=jnp.float32
    )


def contract_last(left, right):
    return lax.dot_general(
        left, right, (((1,), (1,)), ((), ())), preferred_element_type=jnp.float32
    )


def arrange(values, selector):
    return jnp.dot(selector, values, preferred_element_type=jnp.float32).astype(jnp.bfloat16)


def on_device(rows_in, upstream, probs, route, live, gate_up, down):
    experts = lax.axis_size("wide")
    rows_dev = rows_in.shape[0]
    slice_width = rows_in.shape[1]
    hidden_width = down.shape[1]
    capacity = rows_dev * 3 // (2 * experts)
    slot_total = experts * capacity
    own_pair = gate_up[0]
    own_down = down[0]
    expert_of = route[:, 0]
    position = lax.iota(jnp.int32, rows_dev)
    inside = position < live[0]
    live_mask = inside.astype(jnp.float32)
    labels = lax.iota(jnp.int32, experts)
    onehot = (expert_of[:, None] == labels[None, :]).astype(jnp.int32)
    local_loads = jnp.sum(onehot * inside.astype(jnp.int32)[:, None], axis=0)
    global_loads = lax.psum(local_loads, "wide").astype(jnp.float32)
    load_share = global_loads / rows_dev
    row_share = jnp.sum(onehot.astype(jnp.float32) * load_share[None, :], axis=1)
    slot_index = jnp.sum((jnp.cumsum(onehot, axis=0) - 1) * onehot, axis=1)
    target = expert_of * capacity + slot_index
    scaled = ((probs * live_mask)[:, None] * upstream.astype(jnp.float32)).astype(jnp.bfloat16)
    dispatch = (target[None, :] == lax.iota(jnp.int32, slot_total)[:, None]).astype(jnp.bfloat16)
    arrived = (
        lax.all_to_all(
            arrange(rows_in, dispatch).reshape(experts, capacity, slice_width),
            "wide",
            split_axis=0,
            concat_axis=0,
            tiled=True,
        ),
        lax.all_to_all(
            arrange(scaled, dispatch).reshape(experts, capacity, slice_width),
            "wide",
            split_axis=0,
            concat_axis=0,
            tiled=True,
        ),
        lax.all_to_all(
            arrange(upstream, dispatch).reshape(experts, capacity, slice_width),
            "wide",
            split_axis=0,
            concat_axis=0,
            tiled=True,
        ),
    )
    token_rows = arrived[0].reshape(slot_total, slice_width)
    scaled_rows = arrived[1].reshape(slot_total, slice_width)
    upward_rows = arrived[2].reshape(slot_total, slice_width)
    preact = jnp.dot(token_rows, own_pair, preferred_element_type=jnp.float32)
    grad_partial = contract_last(scaled_rows, own_down)
    total_rows = preact.shape[0]
    shares = (
        lax.psum_scatter(
            preact.reshape(total_rows, 2, hidden_width), "grp", scatter_dimension=2, tiled=True
        ),
        lax.psum_scatter(
            grad_partial.reshape(total_rows, 1, hidden_width),
            "grp",
            scatter_dimension=2,
            tiled=True,
        ),
    )
    piece_hidden, piece_gate, piece_up = activate(shares[0][:, 0], shares[0][:, 1], shares[1][:, 0])
    joined = (
        lax.all_gather(piece_hidden[:, None, :], "grp", axis=2, tiled=True),
        lax.all_gather(jnp.stack([piece_gate, piece_up], axis=1), "grp", axis=2, tiled=True),
    )
    hidden = joined[0][:, 0]
    grad_gate = joined[1][:, 0]
    grad_up = joined[1][:, 1]
    grad_pair = jnp.concatenate([grad_gate, grad_up], axis=1)
    grad_own = contract_last(grad_pair, own_pair)
    products = jnp.sum(
        jnp.dot(hidden, own_down, preferred_element_type=jnp.float32)
        * upward_rows.astype(jnp.float32),
        axis=1,
    )
    inner_sum = lax.psum(products, "grp").astype(jnp.bfloat16)
    returned = (
        lax.all_to_all(
            grad_own.astype(jnp.bfloat16).reshape(experts, capacity, slice_width),
            "wide",
            split_axis=0,
            concat_axis=0,
            tiled=True,
        ),
        lax.all_to_all(
            inner_sum.reshape(experts, capacity), "wide", split_axis=0, concat_axis=0, tiled=True
        ),
    )
    grad_rows = contract_rows(dispatch, returned[0].reshape(slot_total, slice_width))
    inner_rows = contract_rows(dispatch, returned[1].reshape(slot_total, 1))[:, 0]
    pair_grad = contract_rows(token_rows, grad_pair)
    down_grad = contract_rows(hidden, scaled_rows)
    grad_prob = (live_mask * (inner_rows + BALANCE * row_share)).astype(jnp.bfloat16)
    return (
        grad_rows.astype(jnp.bfloat16),
        grad_prob,
        pair_grad.astype(jnp.bfloat16)[None],
        down_grad.astype(jnp.bfloat16)[None],
    )


def solution(mesh):
    return jax.shard_map(
        on_device,
        mesh=mesh,
        in_specs=(
            P("wide", "grp"),
            P("wide", "grp"),
            P("wide"),
            P("wide", None),
            P("wide"),
            P("wide", "grp", None),
            P("wide", None, "grp"),
        ),
        out_specs=(P("wide", "grp"), P("wide"), P("wide", "grp", None), P("wide", None, "grp")),
        check_vma=False,
    )
```

profile of v0, /device:TPU:0, one launch (start us, length us, event | category | flops | bytes accessed | tf_op | source)
XLA Modules:
  0.0 430.1 jit_solution(13411549200166403789)
XLA Ops:
  8.0 0.7 fusion.25
  8.7 1.1 reduce-window.6
  10.1 0.9 select_reduce_fusion
  11.0 0.7 multiply_add_fusion
  11.7 0.7 fusion.27
  12.3 3.2 convolution_convert_fusion.4
  15.6 70.0 %all_to_all.30 = bf16[8,96,1792]{2,1,0:T(8,128)(2,1)S(1)} all-to-all(bf16[8,96,1792]{2,1,0:T(8,128)(2,1)S(1)} %bitcast.70), channel_id=1, replica_groups=mesh['wide'=8,'grp'=4] {'wide'}, dimensions={0} | all-to-all | bytes 5505024 | tf_op jit(solution)/shard_map/all_to_all | solution.py:67
  85.6 1.6 copy-done.2
  87.1 4.7 %fusion.11 = f32[768,1,1024]{2,0,1:T(8,128)} fusion(bf16[768,1792]{1,0:T(8,128)(2,1)S(1)} %bitcast.65, bf16[1,1024,1792]{2,1,0:T(8,128)(2,1)S(1)} %copy-done.4), kind=kOutput, calls=%fused_computation.18 | convolution fusion | flops 2818572288 | bytes 9568256 | tf_op jit(solution)/shard_map/dot_general | solution.py:27
  91.8 3.2 convolution_convert_fusion.3
  95.0 4.4 %all-to-all-start.1 = ((bf16[8,96,1792]{2,1,0:T(8,128)(2,1)}), bf16[8,96,1792]{2,1,0:T(8,128)(2,1)}, u32[]{:S(2)}, u32[]{:S(2)}) async-start(bf16[8,96,1792]{2,1,0:T(8,128)(2,1)} %bitcast.69), calls=%async_computation.2 | async-start | bytes 5505024 | tf_op jit(solution)/shard_map/all_to_all | solution.py:60
  99.5 10.1 %copy.15 = bf16[2048,1792]{1,0:T(8,128)(2,1)} copy(bf16[2048,1792]{0,1:T(8,128)(2,1)} %bitcast.63) | data formatting | bytes 14680064 | tf_op jit(solution)/shard_map/dot_general | solution.py:85
  109.6 50.9 %all-to-all-done.1 = bf16[8,96,1792]{2,1,0:T(8,128)(2,1)} async-done(((bf16[8,96,1792]{2,1,0:T(8,128)(2,1)}), bf16[8,96,1792]{2,1,0:T(8,128)(2,1)}, u32[]{:S(2)}, u32[]{:S(2)}) %all-to-all-start.1) | async-done | bytes 2752544 | tf_op jit(solution)/shard_map/all_to_all | solution.py:60
  160.5 10.7 %fusion.30 = f32[768,2,1024]{2,0,1:T(8,128)} fusion(bf16[768,1792,1]{1,0,2:T(8,128)(2,1)} %bitcast.11, bf16[2,1024,1792]{2,1,0:T(8,128)(2,1)} %bitcast.64), kind=kOutput, calls=%fused_computation.53 | convolution fusion | flops 5637144576 | bytes 16384000 | tf_op jit(solution)/shard_map/dot_general | solution.py:85
  171.3 57.0 %reduce-scatter.5.cloned.1.call-done = f32[768,2,256]{2,0,1:T(8,128)} async-done(((f32[768,2,1024]{2,0,1:T(8,128)}), f32[768,2,256]{2,0,1:T(8,128)}) %reduce-scatter.5.cloned.1.call-update) | async-done | bytes 1572880 | tf_op jit(solution)/shard_map/reduce_scatter | solution.py:89
  228.3 2.8 multiply_convert_fusion.4
  231.1 4.7 %convolution_convert_fusion.2 = bf16[768,1792]{1,0:T(8,128)(2,1)} fusion(bf16[512,1792]{1,0:T(8,128)(2,1)} %param.8, s32[512]{0:T(512)S(1)} %multiply_add_fusion), kind=kOutput, calls=%fused_computation.11 | convolution fusion | flops 1411055616 | bytes 4589568 | tf_op jit(solution)/shard_map/dot_general | solution.py:33
  235.8 5.5 %all-to-all-start.3 = ((bf16[8,96,1792]{2,1,0:T(8,128)(2,1)}), bf16[8,96,1792]{2,1,0:T(8,128)(2,1)}, u32[]{:S(2)}, u32[]{:S(2)}) async-start(bf16[8,96,1792]{2,1,0:T(8,128)(2,1)} %bitcast.68), calls=%async_computation.5 | async-start | bytes 5505024 | tf_op jit(solution)/shard_map/all_to_all | solution.py:74
  241.5 0.9 pad_maximum_fusion.3
  242.5 61.0 %all-to-all-done.3 = bf16[8,96,1792]{2,1,0:T(8,128)(2,1)} async-done(((bf16[8,96,1792]{2,1,0:T(8,128)(2,1)}), bf16[8,96,1792]{2,1,0:T(8,128)(2,1)}, u32[]{:S(2)}, u32[]{:S(2)}) %all-to-all-start.3) | async-done | bytes 2752544 | tf_op jit(solution)/shard_map/all_to_all | solution.py:74
  303.5 6.4 %fusion.3 = f32[768]{0:T(1024)S(1)} fusion(bf16[768,1792]{1,0:T(8,128)(2,1)} %bitcast.28, bf16[1,1024,1792]{2,1,0:T(8,128)(2,1)} %param.13, bf16[768,1,1024]{2,0,1:T(8,128)(2,1)} %all-gather.5.cloned.1.call-done), kind=kOutput, calls=%fused_computation.5 | convolution fusion | flops 2822700288 | bytes 7998464 | tf_op jit(solution)/shard_map/dot_general | solution.py:110
  310.0 5.9 %psum.14 = bf16[768]{0:T(1024)(128)(2,1)S(1)} all-reduce(f32[768]{0:T(1024)S(1)} %fusion.3), channel_id=1, replica_groups=mesh['wide'=8,'grp'=4] {'grp'}, use_global_device_ids=true, to_apply=%region_6.7 | all-reduce | flops 768 | bytes 4608 | tf_op jit(solution)/shard_map/psum | solution.py:114
  315.9 0.7 all_to_all.24
  316.6 3.6 all-to-all-start.4
  320.3 2.2 slice_bitcast_fusion.1
  322.4 10.3 %fusion.7 = bf16[768,1792]{1,0:T(8,128)(2,1)} fusion(bf16[1,1792,2048]{2,1,0:T(8,128)(2,1)} %param.12, bf16[768,1024]{1,0:T(8,128)(2,1)S(1)} %get-tuple-element.7, bf16[768,1024]{1,0:T(8,128)(2,1)S(1)} %get-tuple-element.6), kind=kOutput, calls=%fused_computation.14 | convolution fusion | flops 5644812288 | bytes 13238272 | tf_op jit(solution)/shard_map/dot_general | solution.py:27
  332.7 6.1 %all-to-all-start.2 = ((bf16[8,96,1792]{2,1,0:T(8,128)(2,1)}), bf16[8,96,1792]{2,1,0:T(8,128)(2,1)}, u32[]{:S(2)}, u32[]{:S(2)}) async-start(bf16[8,96,1792]{2,1,0:T(8,128)(2,1)} %bitcast.67), calls=%async_computation.4 | async-start | bytes 5505024 | tf_op jit(solution)/shard_map/all_to_all | solution.py:116
  338.8 61.7 %psum.15 = s32[8]{0:T(128)S(1)} all-reduce(s32[8]{0:T(128)S(1)} %get-tuple-element.4), channel_id=1, replica_groups=mesh['wide'=8,'grp'=4] {'wide'}, use_global_device_ids=true, to_apply=%region_8.9 | all-reduce | flops 8 | bytes 64 | tf_op jit(solution)/shard_map/psum | solution.py:52
  400.7 7.2 %fusion.10 = bf16[1,1024,1792]{2,1,0:T(8,128)(2,1)} fusion(bf16[768,1792]{1,0:T(8,128)(2,1)} %bitcast.66, bf16[768,1,1024]{2,0,1:T(8,128)(2,1)} %all-gather.5.cloned.1.call-done), kind=kOutput, calls=%fused_computation.15 | convolution fusion | flops 2820407296 | bytes 7995392 | tf_op jit(solution)/shard_map/dot_general | solution.py:21
  408.3 0.6 select_convert_fusion
  408.9 9.9 %fusion.2 = bf16[1,1792,2048]{2,1,0:T(8,128)(2,1)} fusion(bf16[768,1792]{1,0:T(8,128)(2,1)} %bitcast.10, bf16[768,1024]{1,0:T(8,128)(2,1)S(1)} %get-tuple-element.7, bf16[768,1024]{1,0:T(8,128)(2,1)S(1)} %get-tuple-element.6), kind=kOutput, calls=%fused_computation.3 | convolution fusion | flops 5647106048 | bytes 13238272 | tf_op jit(solution)/shard_map/dot_general | solution.py:21
  418.7 4.8 %convolution_convert_fusion.5 = bf16[512,1792]{1,0:T(8,128)(2,1)} fusion(bf16[768,1792]{1,0:T(8,128)(2,1)} %bitcast.18, s32[512]{0:T(512)S(1)} %multiply_add_fusion), kind=kOutput, calls=%fused_computation.17 | convolution fusion | flops 1410596864 | bytes 4589568 | tf_op jit(solution)/shard_map/dot_general | solution.py:21
  (31 shorter events, 1.3 us)
Async XLA Ops:
  7.2 84.7 %copy-start = (bf16[512,1792]{1,0:T(8,128)(2,1)S(1)}, bf16[512,1792]{1,0:T(8,128)(2,1)}, u32[]{:S(2)}) copy-start(bf16[512,1792]{1,0:T(8,128)(2,1)} %param.7) | copy-start | bytes 5505028
  7.2 164.1 %reduce-scatter.3.cloned.1.call-start = ((), (), s32[]{:S(2)}) async-start(), calls=%async_computation.7 | async-start | bytes 3932160 | tf_op jit(solution)/shard_map/reduce_scatter | solution.py:92
  15.6 71.5 %copy-start.4 = (bf16[1,1024,1792]{2,1,0:T(8,128)(2,1)S(1)}, bf16[1,1024,1792]{2,1,0:T(8,128)(2,1)}, u32[]{:S(2)}) copy-start(bf16[1,1024,1792]{2,1,0:T(8,128)(2,1)} %param.13) | copy-start | bytes 11010052
  85.6 1.6 copy-start.2
  95.0 65.5 %all-to-all-start.1 = ((bf16[8,96,1792]{2,1,0:T(8,128)(2,1)}), bf16[8,96,1792]{2,1,0:T(8,128)(2,1)}, u32[]{:S(2)}, u32[]{:S(2)}) async-start(bf16[8,96,1792]{2,1,0:T(8,128)(2,1)} %bitcast.69), calls=%async_computation.2 | async-start | bytes 5505024 | tf_op jit(solution)/shard_map/all_to_all | solution.py:60
  99.5 128.9 %reduce-scatter.5.cloned.1.call-start = ((), (), s32[]{:S(2)}) async-start(), calls=%async_computation.8 | async-start | bytes 7864320 | tf_op jit(solution)/shard_map/reduce_scatter | solution.py:89
  171.2 132.3 %all-gather.5.cloned.1.call-start = ((), (), s32[]{:S(2)}) async-start(), calls=%async_computation.10 | async-start | bytes 1966080 | tf_op jit(solution)/shard_map/all_gather | solution.py:101
  235.8 67.7 %all-to-all-start.3 = ((bf16[8,96,1792]{2,1,0:T(8,128)(2,1)}), bf16[8,96,1792]{2,1,0:T(8,128)(2,1)}, u32[]{:S(2)}, u32[]{:S(2)}) async-start(bf16[8,96,1792]{2,1,0:T(8,128)(2,1)} %bitcast.68), calls=%async_computation.5 | async-start | bytes 5505024 | tf_op jit(solution)/shard_map/all_to_all | solution.py:74
  241.3 79.0 %all-gather.3.cloned.1.call-start = ((), (), s32[]{:S(2)}) async-start(), calls=%async_computation.9 | async-start | bytes 3932160 | tf_op jit(solution)/shard_map/all_gather | solution.py:102
  316.6 16.1 %all-to-all-start.4 = ((bf16[8,1,96]{2,1,0:T(2,128)(2,1)}), bf16[8,1,96]{2,1,0:T(2,128)(2,1)S(1)}, u32[]{:S(2)}, u32[]{:S(2)}) async-start(bf16[8,1,96]{2,1,0:T(2,128)(2,1)} %all_to_all.24), calls=%async_computation.6 | async-start | bytes 8192 | tf_op jit(solution)/shard_map/all_to_all | solution.py:123
  332.7 67.9 %copy-start.3 = (s32[512,1]{0,1:T(1,128)S(1)}, s32[512,1]{0,1:T(1,128)}, u32[]{:S(2)}) copy-start(s32[512,1]{0,1:T(1,128)} %param.10) | copy-start | bytes 6148
  332.7 86.0 %all-to-all-start.2 = ((bf16[8,96,1792]{2,1,0:T(8,128)(2,1)}), bf16[8,96,1792]{2,1,0:T(8,128)(2,1)}, u32[]{:S(2)}, u32[]{:S(2)}) async-start(bf16[8,96,1792]{2,1,0:T(8,128)(2,1)} %bitcast.67), calls=%async_computation.4 | async-start | bytes 5505024 | tf_op jit(solution)/shard_map/all_to_all | solution.py:116
  418.7 4.8 %copy-start.1 = (bf16[512,1792]{1,0:T(8,128)(2,1)S(1)}, bf16[512,1792]{1,0:T(8,128)(2,1)}, u32[]{:S(2)}) copy-start(bf16[512,1792]{1,0:T(8,128)(2,1)} %param.7) | copy-start | bytes 5505028
Sparse Core Ops, SparseCore 0:
  92.0 36.4 reduce-scatter.2
  171.4 56.9 reduce-scatter.4
  231.3 19.8 all-gather.4
  253.1 28.8 all-gather.2
where the time goes:
time: 431 us; the launch traced here: 430 us
  waiting for transfers between devices  169 us (39%)
  blocking collectives  138 us (32%)
  matrix products  65.4 us (15%)
  starting transfers between devices  20 us (5%)
  local copies, waits for them, and re-layouts  14.9 us (3%)
  between operations  14.6 us (3%)
  other arithmetic  8.52 us (2%)
    all_to_all x1, blocking collectives, on_device(): lax.all_to_all(arrange(scaled, dispatch).reshape(experts, capacity, slice...  70 us
    psum x1, blocking collectives, on_device(): global_loads = lax.psum(local_loads, 'wide').astype(jnp.float32)  61.7 us
    all_to_all x1, waiting for transfers between devices, on_device(): lax.all_to_all(arrange(upstream, dispatch).reshape(experts, capacity, sli...  61 us
    reduce_scatter x1, waiting for transfers between devices, on_device(): lax.psum_scatter(preact.reshape(total_rows, 2, hidden_width), 'grp', scat...  57 us
    all_to_all x1, waiting for transfers between devices, on_device(): lax.all_to_all(arrange(rows_in, dispatch).reshape(experts, capacity, slic...  50.9 us
    dot_general x4, matrix products, contract_rows(): lax.dot_general(left, right, (((0,), (0,)), ((), ())), preferred_element_...  22.2 us
    dot_general x2, matrix products, contract_last(): lax.dot_general(left, right, (((1,), (1,)), ((), ())), preferred_element_...  15 us
    dot_general x3, matrix products, arrange(): jnp.dot(selector, values, preferred_element_type=jnp.float32)  11.1 us
  transfers between devices with their start and end apart: 8, of which 3 were waited for; matrix products, arithmetic and copies ran while one was open for 16% of the time, Pallas kernels for 0%

commit v1 on v0

v1 whole, which is shorter than its diff:
```python
import jax
import jax.numpy as jnp
from jax import lax
from jax.experimental import pallas as pl
from jax.experimental.pallas import tpu as pltpu
from jax.sharding import PartitionSpec as P


BALANCE = 1.0
CHUNKS = 3


def contract_rows(left, right):
    return lax.dot_general(
        left, right, (((0,), (0,)), ((), ())), preferred_element_type=jnp.float32
    )


def contract_last(left, right):
    return lax.dot_general(
        left, right, (((1,), (1,)), ((), ())), preferred_element_type=jnp.float32
    )


def swap(value, axis, members, bits):
    return lax.ppermute(value, axis, [(i, i ^ bits) for i in range(members)])


def halve(parts, index, members):
    bit = 1
    while bit < members:
        upper = (index & bit) != 0
        half = parts[0].shape[1] // 2
        sent = jnp.stack([jnp.where(upper, v[:, :half], v[:, half:]) for v in parts])
        arrived = swap(sent, "grp", members, bit)
        kept = [jnp.where(upper, v[:, half:], v[:, :half]) for v in parts]
        parts = [k.astype(jnp.float32) + a.astype(jnp.float32) for k, a in zip(kept, arrived)]
        bit *= 2
        if bit < members:
            parts = [v.astype(jnp.bfloat16) for v in parts]
    return parts


def double(parts, index, members):
    bit = members // 2
    while bit > 1:
        upper = (index & bit) != 0
        arrived = swap(jnp.stack(parts), "grp", members, bit)
        parts = [
            jnp.concatenate([jnp.where(upper, a, v), jnp.where(upper, v, a)], axis=1)
            for v, a in zip(parts, arrived)
        ]
        bit //= 2
    own = jnp.stack(parts)
    return own, swap(own, "grp", members, bit)


def finish_kernel(index_ref, own_ref, arrived_ref, pair_ref, grad_ref, wide_ref, hidden_ref):
    half = own_ref.shape[2]

    @pl.when(pl.program_id(0) == 0)
    def _():
        upper = (index_ref[0] & 1) != 0
        for kind in range(3):
            target = hidden_ref if kind == 2 else wide_ref
            base = 2 * half * (kind % 2)

            @pl.when(upper)
            def _():
                target[:, base : base + half] = arrived_ref[kind]
                target[:, base + half : base + 2 * half] = own_ref[kind]

            @pl.when(jnp.logical_not(upper))
            def _():
                target[:, base : base + half] = own_ref[kind]
                target[:, base + half : base + 2 * half] = arrived_ref[kind]

    grad_ref[...] = contract_last(wide_ref[...], pair_ref[...]).astype(jnp.bfloat16)


def tile_of(width):
    return 256 if width % 256 == 0 else width


def finish(index, own, arrived, own_pair):
    kinds, rows, half = own.shape
    width = own_pair.shape[0]
    tile = tile_of(width)
    whole = pl.BlockSpec((kinds, rows, half), lambda i, s: (0, 0, 0))
    return pl.pallas_call(
        finish_kernel,
        grid_spec=pltpu.PrefetchScalarGridSpec(
            num_scalar_prefetch=1,
            grid=(width // tile,),
            in_specs=[whole, whole, pl.BlockSpec((tile, 4 * half), lambda i, s: (i, 0))],
            out_specs=[
                pl.BlockSpec((rows, tile), lambda i, s: (0, i)),
                pl.BlockSpec((rows, 4 * half), lambda i, s: (0, 0)),
                pl.BlockSpec((rows, 2 * half), lambda i, s: (0, 0)),
            ],
        ),
        out_shape=[
            jax.ShapeDtypeStruct((rows, width), jnp.bfloat16),
            jax.ShapeDtypeStruct((rows, 4 * half), jnp.bfloat16),
            jax.ShapeDtypeStruct((rows, 2 * half), jnp.bfloat16),
        ],
        cost_estimate=pl.CostEstimate(
            flops=8 * rows * width * half, bytes_accessed=8 * width * half, transcendentals=0
        ),
        name="finish",
    )(index.reshape(1), own, arrived, own_pair)


def weights_kernel(*refs):
    scaled, tokens = refs[:CHUNKS], refs[CHUNKS : 2 * CHUNKS]
    pairs, hiddens = refs[2 * CHUNKS : 3 * CHUNKS], refs[3 * CHUNKS : 4 * CHUNKS]
    pair_ref, down_ref = refs[4 * CHUNKS :]
    pair_total = sum(contract_rows(t[...], p[...]) for t, p in zip(tokens, pairs))
    pair_ref[...] = pair_total.astype(jnp.bfloat16)
    down_total = sum(contract_rows(h[...], v[...]) for h, v in zip(hiddens, scaled))
    down_ref[...] = down_total.astype(jnp.bfloat16)


def weight_grads(arrived, pairs, hiddens, width):
    rows = arrived[0].shape[0]
    hidden_width = hiddens[0].shape[1]
    tile = tile_of(width)
    steps = width // tile
    if steps == 1:
        scaled, tokens, shift = (
            [v[:, :width] for v in arrived],
            [v[:, width:] for v in arrived],
            0,
        )
    else:
        scaled, tokens, shift = arrived, arrived, steps
    return pl.pallas_call(
        weights_kernel,
        grid=(steps,),
        in_specs=[pl.BlockSpec((rows, tile), lambda i: (0, i))] * CHUNKS
        + [pl.BlockSpec((rows, tile), lambda i: (0, i + shift))] * CHUNKS
        + [pl.BlockSpec((rows, 2 * hidden_width), lambda i: (0, 0))] * CHUNKS
        + [pl.BlockSpec((rows, hidden_width), lambda i: (0, 0))] * CHUNKS,
        out_specs=[
            pl.BlockSpec((tile, 2 * hidden_width), lambda i: (i, 0)),
            pl.BlockSpec((hidden_width, tile), lambda i: (0, i)),
        ],
        out_shape=[
            jax.ShapeDtypeStruct((width, 2 * hidden_width), jnp.bfloat16),
            jax.ShapeDtypeStruct((hidden_width, width), jnp.bfloat16),
        ],
        cost_estimate=pl.CostEstimate(
            flops=6 * CHUNKS * rows * width * hidden_width,
            bytes_accessed=6 * width * hidden_width,
            transcendentals=0,
        ),
        name="weight_grads",
    )(*scaled, *tokens, *pairs, *hiddens)


def activate(gate, up, grad_hidden):
    sigmoid_gate = jax.nn.sigmoid(gate)
    swish = gate * sigmoid_gate
    hidden = (swish * up).astype(jnp.bfloat16)
    inner = jnp.sum(hidden.astype(jnp.float32) * grad_hidden, axis=1)
    grad_gate = (grad_hidden * up * sigmoid_gate * (1.0 + gate * (1.0 - sigmoid_gate))).astype(
        jnp.bfloat16
    )
    grad_up = (grad_hidden * swish).astype(jnp.bfloat16)
    return [grad_gate, grad_up, hidden], inner


def exchange(values, experts):
    sent = values.reshape(experts, values.shape[0] // experts, values.shape[1])
    got = lax.all_to_all(sent, "wide", split_axis=0, concat_axis=0, tiled=True)
    return got.reshape(values.shape)


def after(value, *others):
    return lax.optimization_barrier((value, *others))[0]


def on_device(rows_in, upstream, probs, route, live, gate_up, down):
    experts = lax.axis_size("wide")
    members = lax.axis_size("grp")
    index = lax.axis_index("grp")
    rows_dev, width = rows_in.shape
    hidden_width = down.shape[1]
    capacity = rows_dev * 3 // (2 * experts)
    depth = capacity // CHUNKS
    chunk_rows = experts * depth
    own_pair = gate_up[0]
    own_down = down[0]
    expert_of = route[:, 0]
    inside = lax.iota(jnp.int32, rows_dev) < live[0]
    live_mask = inside.astype(jnp.float32)
    labels = lax.iota(jnp.int32, experts)
    onehot = (expert_of[:, None] == labels[None, :]).astype(jnp.int32)
    slot = jnp.sum((jnp.cumsum(onehot, axis=0) - 1) * onehot, axis=1)
    scaled = ((probs * live_mask)[:, None] * upstream.astype(jnp.float32)).astype(jnp.bfloat16)
    both = jnp.concatenate([scaled, rows_in], axis=1)
    target = (slot // depth) * chunk_rows + expert_of * depth + slot % depth

    def arrange(step):
        places = lax.iota(jnp.int32, chunk_rows) + step * chunk_rows
        select = (target[None, :] == places[:, None]).astype(jnp.bfloat16)
        dispatch.append(select)
        return jnp.dot(select, both, preferred_element_type=jnp.float32).astype(jnp.bfloat16)

    def project(block):
        grad_part = contract_last(block[:, :width], own_down).astype(jnp.bfloat16)
        pre_part = jnp.dot(block[:, width:], own_pair, preferred_element_type=jnp.float32)
        pre_part = pre_part.astype(jnp.bfloat16)
        return [pre_part[:, :hidden_width], pre_part[:, hidden_width:], grad_part]

    dispatch, pairs, hiddens, inners = [], [], [], []
    sent = [arrange(step) for step in range(CHUNKS)]
    arrived, parts, returned = [], [], []
    for step in range(CHUNKS):
        if step > 0:
            sent[step] = after(sent[step], arrived[step - 1])
        arrived.append(exchange(sent[step], experts))
        parts.append(project(arrived[step]))
    packed = [None] * CHUNKS
    for step in range(CHUNKS):
        share = halve(parts[step], index, members)
        packed[step], inner = activate(*share)
        inners.append(inner)
    inner_all = jnp.stack(inners, axis=0)
    bit = 1
    while bit < members:
        inner_all = inner_all + swap(inner_all, "grp", members, bit)
        bit *= 2
    local_loads = jnp.sum(onehot * inside.astype(jnp.int32)[:, None], axis=0)
    digits = jnp.concatenate([local_loads // 16, local_loads % 16])
    digits = jnp.broadcast_to(digits.astype(jnp.bfloat16)[None, :], (chunk_rows, 2 * experts))
    extra = jnp.concatenate([inner_all.T.astype(jnp.bfloat16), digits], axis=1)
    extra = jnp.pad(extra, ((0, 0), (0, 128 - extra.shape[1])))
    for step in range(CHUNKS):
        if step == CHUNKS - 1:
            packed[step] = [after(v, returned[0]) for v in packed[step]]
        own, other = double(packed[step], index, members)
        grad_own, grad_pair, hidden = finish(index, own, other, own_pair)
        pairs.append(grad_pair)
        hiddens.append(hidden)
        if step == CHUNKS - 1:
            grad_own = jnp.concatenate([grad_own, extra], axis=1)
        returned.append(exchange(grad_own, experts))

    pair_grad, down_grad = weight_grads(arrived, pairs, hiddens, width)

    tail = returned[-1][:, width:].astype(jnp.float32)
    returned[-1] = returned[-1][:, :width]
    counts = tail.reshape(experts, depth, 128)[:, 0, CHUNKS : CHUNKS + 2 * experts]
    load_share = jnp.sum(counts[:, :experts] * 16 + counts[:, experts:], axis=0) / rows_dev
    hot = (
        (expert_of * depth + slot % depth)[:, None] == lax.iota(jnp.int32, chunk_rows)[None, :]
    ).astype(jnp.float32)
    inner_rows = jnp.zeros((rows_dev,), jnp.float32)
    for step in range(CHUNKS):
        found = jnp.sum(hot * tail[:, step][None, :], axis=1)
        inner_rows = jnp.where(slot // depth == step, found, inner_rows)
    inner_rows = (inner_rows / probs).astype(jnp.bfloat16).astype(jnp.float32)
    row_share = jnp.sum(onehot.astype(jnp.float32) * load_share[None, :], axis=1)
    grad_prob = (live_mask * (inner_rows + BALANCE * row_share)).astype(jnp.bfloat16)

    grad_rows = None
    for step in range(CHUNKS):
        part = contract_rows(dispatch[step], returned[step]).astype(jnp.bfloat16)
        grad_rows = part if grad_rows is None else grad_rows + part
    return grad_rows, grad_prob, pair_grad[None], down_grad[None]


def solution(mesh):
    return jax.shard_map(
        on_device,
        mesh=mesh,
        in_specs=(
            P("wide", "grp"),
            P("wide", "grp"),
            P("wide"),
            P("wide", None),
            P("wide"),
            P("wide", "grp", None),
            P("wide", None, "grp"),
        ),
        out_specs=(P("wide", "grp"), P("wide"), P("wide", "grp", None), P("wide", None, "grp")),
        check_vma=False,
    )
```

time: 431 us -> 280 us (0.65)
  blocking collectives: 138 us -> 0 us
  Pallas kernels: 0 us -> 38.9 us
  waiting for transfers between devices: 169 us -> 138 us
  matrix products: 65.4 us -> 40.6 us
  starting transfers between devices: 20 us -> 37.1 us
  between operations: 14.6 us -> 2.04 us
  local copies, waits for them, and re-layouts: 14.9 us -> 2.51 us
  other arithmetic: 8.52 us -> 18.9 us
    all_to_all x1 -> x0, blocking collectives: 70 us -> none  [on_device(): lax.all_to_all(arrange(scaled, dispatch).reshape(experts, capacity, slice...]
    psum x2 -> x0, blocking collectives: 67.7 us -> none  [the longest x1 61.7 us: on_device(): global_loads = lax.psum(local_loads, 'wide').astype(jnp.float32)]
    reduce_scatter x2 -> x0, waiting for transfers between devices: 57 us -> none  [the longest x1 57 us: on_device(): lax.psum_scatter(preact.reshape(total_rows, 2, hidden_width), 'grp', scat...]
    ppermute x0 -> x14, waiting for transfers between devices: none -> 41.1 us  [swap(): return lax.ppermute(value, axis, [(i, i ^ bits) for i in range(members)])]
    pallas_call x0 -> x4, Pallas kernels: none -> 38.9 us  [the longest x3 25.1 us: finish(): pl.pallas_call(finish_kernel, grid_spec=pltpu.PrefetchScalarGridSpec(num_...]
    dot_general x4 -> x3, matrix products: 22.2 us -> 4.93 us  [contract_rows(): lax.dot_general(left, right, (((0,), (0,)), ((), ())), preferred_element_...]
    all_to_all x4 -> x6, waiting for transfers between devices: 112 us -> 97.2 us  [exchange(): got = lax.all_to_all(sent, 'wide', split_axis=0, concat_axis=0, tiled=True)]
    dot_general x1 -> x0, local copies, waits for them, and re-layouts: 10.1 us -> none  [on_device(): preact = jnp.dot(token_rows, own_pair, preferred_element_type=jnp.float32)]
  transfers between devices with their start and end apart: 8 -> 20, of which waited for: 3 -> 12; matrix products, arithmetic and copies ran while one was open for 16% -> 14% of each run, Pallas kernels for 0% -> 14%
where the time goes in v1:
time: 280 us; the launch traced here: 278 us
  waiting for transfers between devices  138 us (49%)
  matrix products  40.6 us (14%)
  Pallas kernels  38.9 us (14%)
  starting transfers between devices  37.1 us (13%)
  other arithmetic  18.9 us (7%)
    all_to_all x6, waiting for transfers between devices, exchange(): got = lax.all_to_all(sent, 'wide', split_axis=0, concat_axis=0, tiled=True)  97.2 us
    ppermute x14, waiting for transfers between devices, swap(): return lax.ppermute(value, axis, [(i, i ^ bits) for i in range(members)])  41.1 us
    all_to_all x6, starting transfers between devices, exchange(): got = lax.all_to_all(sent, 'wide', split_axis=0, concat_axis=0, tiled=True)  27.1 us
    pallas_call x3, Pallas kernels, finish(): pl.pallas_call(finish_kernel, grid_spec=pltpu.PrefetchScalarGridSpec(num_...  25.1 us
    dot_general x3, matrix products, project(): jnp.dot(block[:, width:], own_pair, preferred_element_type=jnp.float32)  16.3 us
    pallas_call x1, Pallas kernels, weight_grads(): pl.pallas_call(weights_kernel, grid=(steps,), in_specs=[pl.BlockSpec((row...  13.8 us
    dot_general x3, matrix products, contract_last(): lax.dot_general(left, right, (((1,), (1,)), ((), ())), preferred_element_...  10.1 us
    ppermute x14, starting transfers between devices, swap(): return lax.ppermute(value, axis, [(i, i ^ bits) for i in range(members)])  10 us
  transfers between devices with their start and end apart: 20, of which 12 were waited for; matrix products, arithmetic and copies ran while one was open for 14% of the time, Pallas kernels for 14%

profile of v1, /device:TPU:0, one launch (start us, length us, event | category | flops | bytes accessed | tf_op | source)
XLA Modules:
  0.0 278.4 jit_solution(10232953950567883941)
XLA Ops:
  7.7 2.4 convolution_convert_fusion.2
  10.0 7.3 %all-to-all-start = ((bf16[8,32,3584]{2,1,0:T(8,128)(2,1)}), bf16[8,32,3584]{2,1,0:T(8,128)(2,1)S(1)}, u32[]{:S(2)}, u32[]{:S(2)}) async-start(bf16[8,32,3584]{2,1,0:T(8,128)(2,1)} %bitcast.321), calls=%async_computation | async-start | bytes 3670016 | tf_op jit(solution)/shard_map/all_to_all | solution.py:175
  17.3 4.4 %convolution_convert_fusion.1 = bf16[256,3584]{1,0:T(8,128)(2,1)} fusion(bf16[512,1792]{1,0:T(8,128)(2,1)} %param.7, bf16[512,1792]{1,0:T(8,128)(2,1)} %copy-done.7, s32[512]{0:T(512)S(1)} %fusion.55, s32[256]{0:T(256)S(1)} %iota_add_fusion.1), kind=kOutput, calls=%fused_computation.1 | convolution fusion | flops 947912704 | bytes 5508096 | tf_op jit(solution)/shard_map/dot_general | solution.py:208
  21.8 38.2 %all-to-all-done = bf16[8,32,3584]{2,1,0:T(8,128)(2,1)S(1)} async-done(((bf16[8,32,3584]{2,1,0:T(8,128)(2,1)}), bf16[8,32,3584]{2,1,0:T(8,128)(2,1)S(1)}, u32[]{:S(2)}, u32[]{:S(2)}) %all-to-all-start) | async-done | bytes 1835040 | tf_op jit(solution)/shard_map/all_to_all | solution.py:175
  59.9 4.3 %all-to-all-start.2 = ((bf16[8,32,3584]{2,1,0:T(8,128)(2,1)}), bf16[8,32,3584]{2,1,0:T(8,128)(2,1)}, u32[]{:S(2)}, u32[]{:S(2)}) async-start(bf16[8,32,3584]{2,1,0:T(8,128)(2,1)} %bitcast.320), calls=%async_computation.2 | async-start | bytes 3670016 | tf_op jit(solution)/shard_map/all_to_all | solution.py:175
  64.3 3.2 %fusion.9 = bf16[256,1024]{1,0:T(8,128)(2,1)S(1)} fusion(bf16[1,1024,1792]{2,1,0:T(8,128)(2,1)} %param.13, bf16[256,3584]{1,0:T(8,128)(2,1)S(1)} %bitcast.315), kind=kOutput, calls=%fused_computation.21 | convolution fusion | flops 939786240 | bytes 5111808 | tf_op jit(solution)/shard_map/dot_general | solution.py:20
  67.5 5.4 %convolution_convert_fusion.8 = bf16[256,2048]{1,0:T(8,128)(2,1)S(1)} fusion(bf16[256,3584]{1,0:T(8,128)(2,1)} %bitcast.316, bf16[1,1792,2048]{2,1,0:T(8,128)(2,1)} %param.12), kind=kOutput, calls=%fused_computation.18 | convolution fusion | flops 1879572480 | bytes 9306112 | tf_op jit(solution)/shard_map/dot_general | solution.py:212
  73.2 2.4 collective-permute-done
  78.7 2.4 convolution_convert_fusion
  81.2 7.2 %collective-permute-done.1 = bf16[3,256,256]{2,1,0:T(8,128)(2,1)S(1)} collective-permute-done((bf16[3,256,256]{2,1,0:T(8,128)(2,1)S(1)}, bf16[3,256,256]{2,1,0:T(8,128)(2,1)S(1)}, u32[]{:S(2)}, u32[]{:S(2)}) %collective-permute-start.1) | collective-permute-done | bytes 393248 | tf_op jit(solution)/shard_map/ppermute | solution.py:26
  88.6 17.9 %all-to-all-done.2 = bf16[8,32,3584]{2,1,0:T(8,128)(2,1)} async-done(((bf16[8,32,3584]{2,1,0:T(8,128)(2,1)}), bf16[8,32,3584]{2,1,0:T(8,128)(2,1)}, u32[]{:S(2)}, u32[]{:S(2)}) %all-to-all-start.2) | async-done | bytes 1835040 | tf_op jit(solution)/shard_map/all_to_all | solution.py:175
  106.5 3.5 %fusion.12 = bf16[256,1024]{1,0:T(8,128)(2,1)S(1)} fusion(bf16[1,1024,1792]{2,1,0:T(8,128)(2,1)} %param.13, bf16[256,3584]{1,0:T(8,128)(2,1)} %bitcast.34.refs_1_.refs_4_), kind=kOutput, calls=%fused_computation.22 | convolution fusion | flops 939786240 | bytes 5111808 | tf_op jit(solution)/shard_map/dot_general | solution.py:20
  110.0 5.4 %convolution_convert_fusion.7 = bf16[256,2048]{1,0:T(8,128)(2,1)S(1)} fusion(bf16[256,3584]{1,0:T(8,128)(2,1)} %bitcast.34.refs_1_.refs_4_, bf16[1,1792,2048]{2,1,0:T(8,128)(2,1)} %param.12), kind=kOutput, calls=%fused_computation.17 | convolution fusion | flops 1879572480 | bytes 9306112 | tf_op jit(solution)/shard_map/dot_general | solution.py:212
  115.4 4.5 %all-to-all-start.4 = ((bf16[8,32,3584]{2,1,0:T(8,128)(2,1)}), bf16[8,32,3584]{2,1,0:T(8,128)(2,1)}, u32[]{:S(2)}, u32[]{:S(2)}) async-start(bf16[8,32,3584]{2,1,0:T(8,128)(2,1)} %bitcast.319), calls=%async_computation.4 | async-start | bytes 3670016 | tf_op jit(solution)/shard_map/all_to_all | solution.py:175
  122.2 10.0 %collective-permute-done.2 = bf16[3,256,256]{2,1,0:T(8,128)(2,1)S(1)} collective-permute-done((bf16[3,256,256]{2,1,0:T(8,128)(2,1)S(1)}, bf16[3,256,256]{2,1,0:T(8,128)(2,1)S(1)}, u32[]{:S(2)}, u32[]{:S(2)}) %collective-permute-start.2) | collective-permute-done | bytes 393248 | tf_op jit(solution)/shard_map/ppermute | solution.py:26
  134.5 9.0 %collective-permute-done.5 = bf16[3,256,256]{2,1,0:T(8,128)(2,1)S(1)} collective-permute-done((bf16[3,256,256]{2,1,0:T(8,128)(2,1)S(1)}, bf16[3,256,256]{2,1,0:T(8,128)(2,1)S(1)}, u32[]{:S(2)}, u32[]{:S(2)}) %collective-permute-start.5) | collective-permute-done | bytes 393248 | tf_op jit(solution)/shard_map/ppermute | solution.py:26
  144.0 18.0 %all-to-all-done.4 = bf16[8,32,3584]{2,1,0:T(8,128)(2,1)} async-done(((bf16[8,32,3584]{2,1,0:T(8,128)(2,1)}), bf16[8,32,3584]{2,1,0:T(8,128)(2,1)}, u32[]{:S(2)}, u32[]{:S(2)}) %all-to-all-start.4) | async-done | bytes 1835040 | tf_op jit(solution)/shard_map/all_to_all | solution.py:175
  162.1 3.5 %fusion.15 = bf16[256,1024]{1,0:T(8,128)(2,1)S(1)} fusion(bf16[1,1024,1792]{2,1,0:T(8,128)(2,1)} %param.13, bf16[256,3584]{1,0:T(8,128)(2,1)} %bitcast.59.refs_2_.refs_5_), kind=kOutput, calls=%fused_computation.23 | convolution fusion | flops 939786240 | bytes 5111808 | tf_op jit(solution)/shard_map/dot_general | solution.py:20
  165.6 5.4 %convolution_convert_fusion.6 = bf16[256,2048]{1,0:T(8,128)(2,1)S(1)} fusion(bf16[256,3584]{1,0:T(8,128)(2,1)} %bitcast.59.refs_2_.refs_5_, bf16[1,1792,2048]{2,1,0:T(8,128)(2,1)} %param.12), kind=kOutput, calls=%fused_computation.16 | convolution fusion | flops 1879572480 | bytes 9306112 | tf_op jit(solution)/shard_map/dot_general | solution.py:212
  173.7 8.4 %finish.3 = (bf16[256,1792]{1,0:T(8,128)(2,1)}, bf16[256,2048]{1,0:T(8,128)(2,1)}, bf16[256,1024]{1,0:T(8,128)(2,1)}) custom-call(s32[1]{0:T(128)} %bitcast.4.index_ref, bf16[3,256,512]{2,1,0:T(8,128)(2,1)} %copy-done.3, bf16[3,256,512]{2,1,0:T(8,128)(2,1)} %collective-permute-done.3.arrived_ref, bf16[1792,2048]{1,0:T(8,128)(2,1)} %bitcast.307), custom_call_target="tpu_custom_call" | custom-call | flops 1879048192 | bytes 7340032 | tf_op jit(solution)/shard_map/finish/pallas_call | solution.py:90
  182.1 3.6 %all-to-all-start.1 = ((bf16[8,32,1792]{2,1,0:T(8,128)(2,1)}), bf16[8,32,1792]{2,1,0:T(8,128)(2,1)S(1)}, u32[]{:S(2)}, u32[]{:S(2)}) async-start(bf16[8,32,1792]{2,1,0:T(8,128)(2,1)} %bitcast.332), calls=%async_computation.1 | async-start | bytes 1835008 | tf_op jit(solution)/shard_map/all_to_all | solution.py:175
  189.1 10.5 %collective-permute-done.9 = bf16[3,256,256]{2,1,0:T(8,128)(2,1)S(1)} collective-permute-done((bf16[3,256,256]{2,1,0:T(8,128)(2,1)S(1)}, bf16[3,256,256]{2,1,0:T(8,128)(2,1)S(1)}, u32[]{:S(2)}, u32[]{:S(2)}) %collective-permute-start.9) | collective-permute-done | bytes 393248 | tf_op jit(solution)/shard_map/ppermute | solution.py:26
  200.2 9.0 %all-to-all-done.1 = bf16[8,32,1792]{2,1,0:T(8,128)(2,1)S(1)} async-done(((bf16[8,32,1792]{2,1,0:T(8,128)(2,1)}), bf16[8,32,1792]{2,1,0:T(8,128)(2,1)S(1)}, u32[]{:S(2)}, u32[]{:S(2)}) %all-to-all-start.1) | async-done | bytes 917536 | tf_op jit(solution)/shard_map/all_to_all | solution.py:175
  210.7 8.4 %finish.4 = (bf16[256,1792]{1,0:T(8,128)(2,1)}, bf16[256,2048]{1,0:T(8,128)(2,1)}, bf16[256,1024]{1,0:T(8,128)(2,1)}) custom-call(s32[1]{0:T(128)} %bitcast.4.index_ref, bf16[3,256,512]{2,1,0:T(8,128)(2,1)} %copy-done.5, bf16[3,256,512]{2,1,0:T(8,128)(2,1)} %copy-done.10, bf16[1792,2048]{1,0:T(8,128)(2,1)} %bitcast.308), custom_call_target="tpu_custom_call" | custom-call | flops 1879048192 | bytes 7340032 | tf_op jit(solution)/shard_map/finish/pallas_call | solution.py:90
  219.1 3.6 %all-to-all-start.3 = ((bf16[8,32,1792]{2,1,0:T(8,128)(2,1)}), bf16[8,32,1792]{2,1,0:T(8,128)(2,1)S(1)}, u32[]{:S(2)}, u32[]{:S(2)}) async-start(bf16[8,32,1792]{2,1,0:T(8,128)(2,1)} %bitcast.331), calls=%async_computation.3 | async-start | bytes 1835008 | tf_op jit(solution)/shard_map/all_to_all | solution.py:175
  229.4 8.4 %finish.5 = (bf16[256,1792]{1,0:T(8,128)(2,1)}, bf16[256,2048]{1,0:T(8,128)(2,1)}, bf16[256,1024]{1,0:T(8,128)(2,1)}) custom-call(s32[1]{0:T(128)} %bitcast.4.index_ref, bf16[3,256,512]{2,1,0:T(8,128)(2,1)} %copy-done.4, bf16[3,256,512]{2,1,0:T(8,128)(2,1)} %copy-done.9, bf16[1792,2048]{1,0:T(8,128)(2,1)} %bitcast.309), custom_call_target="tpu_custom_call" | custom-call | flops 1879048192 | bytes 7340032 | tf_op jit(solution)/shard_map/finish/pallas_call | solution.py:90
  237.8 2.2 fusion.18
  240.0 5.7 %all-to-all-done.3 = bf16[8,32,1792]{2,1,0:T(8,128)(2,1)S(1)} async-done(((bf16[8,32,1792]{2,1,0:T(8,128)(2,1)}), bf16[8,32,1792]{2,1,0:T(8,128)(2,1)S(1)}, u32[]{:S(2)}, u32[]{:S(2)}) %all-to-all-start.3) | async-done | bytes 917536 | tf_op jit(solution)/shard_map/all_to_all | solution.py:175
  245.7 3.8 %all-to-all-start.5 = ((bf16[8,32,1920]{2,1,0:T(8,128)(2,1)}), bf16[8,32,1920]{2,1,0:T(8,128)(2,1)S(1)}, u32[]{:S(2)}, u32[]{:S(2)}) async-start(bf16[8,32,1920]{2,1,0:T(8,128)(2,1)} %bitcast.85), calls=%async_computation.5 | async-start | bytes 1966080 | tf_op jit(solution)/shard_map/all_to_all | solution.py:175
  251.5 13.8 %weight_grads.1 = (bf16[1792,2048]{1,0:T(8,128)(2,1)}, bf16[1024,1792]{1,0:T(8,128)(2,1)}) custom-call(bf16[256,3584]{1,0:T(8,128)(2,1)} %bitcast.317, bf16[256,3584]{1,0:T(8,128)(2,1)} %bitcast.34.refs_1_.refs_4_, bf16[256,3584]{1,0:T(8,128)(2,1)} %bitcast.59.refs_2_.refs_5_, bf16[256,3584]{1,0:T(8,128)(2,1)} %bitcast.318, ...), custom_call_target="tpu_custom_call" | custom-call | flops 8455716864 | bytes 11010048 | tf_op jit(solution)/shard_map/weight_grads/pallas_call | solution.py:137
  265.3 8.5 %all-to-all-done.5 = bf16[8,32,1920]{2,1,0:T(8,128)(2,1)S(1)} async-done(((bf16[8,32,1920]{2,1,0:T(8,128)(2,1)}), bf16[8,32,1920]{2,1,0:T(8,128)(2,1)S(1)}, u32[]{:S(2)}, u32[]{:S(2)}) %all-to-all-start.5) | async-done | bytes 983072 | tf_op jit(solution)/shard_map/all_to_all | solution.py:175
  275.2 2.1 fusion.7
  (128 shorter events, 34.1 us)
Async XLA Ops:
  0.6 7.0 %copy-start.13 = (bf16[512,1792]{1,0:T(8,128)(2,1)S(1)}, bf16[512,1792]{1,0:T(8,128)(2,1)}, u32[]{:S(2)}) copy-start(bf16[512,1792]{1,0:T(8,128)(2,1)} %param.7) | copy-start | bytes 5505028
  7.6 2.4 copy-start.7
  10.0 49.9 %all-to-all-start = ((bf16[8,32,3584]{2,1,0:T(8,128)(2,1)}), bf16[8,32,3584]{2,1,0:T(8,128)(2,1)S(1)}, u32[]{:S(2)}, u32[]{:S(2)}) async-start(bf16[8,32,3584]{2,1,0:T(8,128)(2,1)} %bitcast.321), calls=%async_computation | async-start | bytes 3670016 | tf_op jit(solution)/shard_map/all_to_all | solution.py:175
  59.9 7.5 %copy-start.6 = (bf16[8,32,3584]{2,1,0:T(8,128)(2,1)}, bf16[8,32,3584]{2,1,0:T(8,128)(2,1)S(1)}, u32[]{:S(2)}) copy-start(bf16[8,32,3584]{2,1,0:T(8,128)(2,1)S(1)} %all-to-all-done) | copy-start | bytes 5505028
  59.9 46.6 %all-to-all-start.2 = ((bf16[8,32,3584]{2,1,0:T(8,128)(2,1)}), bf16[8,32,3584]{2,1,0:T(8,128)(2,1)}, u32[]{:S(2)}, u32[]{:S(2)}) async-start(bf16[8,32,3584]{2,1,0:T(8,128)(2,1)} %bitcast.320), calls=%async_computation.2 | async-start | bytes 3670016 | tf_op jit(solution)/shard_map/all_to_all | solution.py:175
  73.1 2.5 collective-permute-start
  73.2 5.5 %copy-start.8 = (bf16[512,1792]{1,0:T(8,128)(2,1)S(1)}, bf16[512,1792]{1,0:T(8,128)(2,1)}, u32[]{:S(2)}) copy-start(bf16[512,1792]{1,0:T(8,128)(2,1)} %copy-done.7) | copy-start | bytes 5505028
  73.2 5.5 %copy-start.14 = (bf16[512,1792]{1,0:T(8,128)(2,1)S(1)}, bf16[512,1792]{1,0:T(8,128)(2,1)}, u32[]{:S(2)}) copy-start(bf16[512,1792]{1,0:T(8,128)(2,1)} %param.7) | copy-start | bytes 5505028
  77.1 11.2 %collective-permute-start.1 = (bf16[3,256,256]{2,1,0:T(8,128)(2,1)S(1)}, bf16[3,256,256]{2,1,0:T(8,128)(2,1)S(1)}, u32[]{:S(2)}, u32[]{:S(2)}) collective-permute-start(bf16[3,256,256]{2,1,0:T(8,128)(2,1)S(1)} %pad_maximum_fusion.10), channel_id=1, source_target_pairs={{0,2},{1,3},{2,0},{3,1},{4,6},{5,7},{6,4},{7,5},{8,10},{9,11},{10,... | collective-permute-start | bytes 1179656 | tf_op jit(solution)/shard_map/ppermute | solution.py:26
  115.4 46.6 %all-to-all-start.4 = ((bf16[8,32,3584]{2,1,0:T(8,128)(2,1)}), bf16[8,32,3584]{2,1,0:T(8,128)(2,1)}, u32[]{:S(2)}, u32[]{:S(2)}) async-start(bf16[8,32,3584]{2,1,0:T(8,128)(2,1)} %bitcast.319), calls=%async_computation.4 | async-start | bytes 3670016 | tf_op jit(solution)/shard_map/all_to_all | solution.py:175
  120.1 12.1 %collective-permute-start.4 = (bf16[3,256,512]{2,1,0:T(8,128)(2,1)S(1)}, bf16[3,256,512]{2,1,0:T(8,128)(2,1)S(1)}, u32[]{:S(2)}, u32[]{:S(2)}) collective-permute-start(bf16[3,256,512]{2,1,0:T(8,128)(2,1)S(1)} %pad_maximum_fusion.6), channel_id=1, source_target_pairs={{0,1},{1,0},{2,3},{3,2},{4,5},{5,4},{6,7},{7,6},{8,9},{9,8},{10,11... | collective-permute-start | bytes 2359304 | tf_op jit(solution)/shard_map/ppermute | solution.py:26
  120.6 11.6 %collective-permute-start.2 = (bf16[3,256,256]{2,1,0:T(8,128)(2,1)S(1)}, bf16[3,256,256]{2,1,0:T(8,128)(2,1)S(1)}, u32[]{:S(2)}, u32[]{:S(2)}) collective-permute-start(bf16[3,256,256]{2,1,0:T(8,128)(2,1)S(1)} %pad_maximum_fusion.11), channel_id=1, source_target_pairs={{0,2},{1,3},{2,0},{3,1},{4,6},{5,7},{6,4},{7,5},{8,10},{9,11},{10,... | collective-permute-start | bytes 1179656 | tf_op jit(solution)/shard_map/ppermute | solution.py:26
  132.7 10.8 %collective-permute-start.5 = (bf16[3,256,256]{2,1,0:T(8,128)(2,1)S(1)}, bf16[3,256,256]{2,1,0:T(8,128)(2,1)S(1)}, u32[]{:S(2)}, u32[]{:S(2)}) collective-permute-start(bf16[3,256,256]{2,1,0:T(8,128)(2,1)S(1)} %pad_maximum_fusion.12), channel_id=1, source_target_pairs={{0,2},{1,3},{2,0},{3,1},{4,6},{5,7},{6,4},{7,5},{8,10},{9,11},{10,... | collective-permute-start | bytes 1179656 | tf_op jit(solution)/shard_map/ppermute | solution.py:26
  134.4 31.1 %copy-start.3 = (bf16[3,256,512]{2,1,0:T(8,128)(2,1)}, bf16[3,256,512]{2,1,0:T(8,128)(2,1)S(1)}, u32[]{:S(2)}) copy-start(bf16[3,256,512]{2,1,0:T(8,128)(2,1)S(1)} %pad_maximum_fusion.5.own_ref) | copy-start | bytes 2359300
  134.4 39.3 %collective-permute-start.3 = (bf16[3,256,512]{2,1,0:T(8,128)(2,1)S(1)}, bf16[3,256,512]{2,1,0:T(8,128)(2,1)}, u32[]{:S(2)}, u32[]{:S(2)}) collective-permute-start(bf16[3,256,512]{2,1,0:T(8,128)(2,1)S(1)} %pad_maximum_fusion.5.own_ref), channel_id=1, source_target_pairs={{0,1},{1,0},{2,3},{3,2},{4,5},{5,4},{6,7},{7,6},{8,9},{9,8},{10,11... | collective-permute-start | bytes 2359304 | tf_op jit(solution)/shard_map/ppermute | solution.py:26
  172.1 14.7 %collective-permute-start.8 = (bf16[3,256,512]{2,1,0:T(8,128)(2,1)}, bf16[3,256,512]{2,1,0:T(8,128)(2,1)}, u32[]{:S(2)}, u32[]{:S(2)}) collective-permute-start(bf16[3,256,512]{2,1,0:T(8,128)(2,1)} %pad_maximum_fusion.8), channel_id=1, source_target_pairs={{0,1},{1,0},{2,3},{3,2},{4,5},{5,4},{6,7},{7,6},{8,9},{9,8},{10,11... | collective-permute-start | bytes 2359304 | tf_op jit(solution)/shard_map/ppermute | solution.py:26
  172.1 13.5 %collective-permute-start.6 = (bf16[3,256,256]{2,1,0:T(8,128)(2,1)S(1)}, bf16[3,256,256]{2,1,0:T(8,128)(2,1)}, u32[]{:S(2)}, u32[]{:S(2)}) collective-permute-start(bf16[3,256,256]{2,1,0:T(8,128)(2,1)S(1)} %pad_maximum_fusion.13), channel_id=1, source_target_pairs={{0,2},{1,3},{2,0},{3,1},{4,6},{5,7},{6,4},{7,5},{8,10},{9,11},{10,... | collective-permute-start | bytes 1179656 | tf_op jit(solution)/shard_map/ppermute | solution.py:26
  182.1 27.1 %all-to-all-start.1 = ((bf16[8,32,1792]{2,1,0:T(8,128)(2,1)}), bf16[8,32,1792]{2,1,0:T(8,128)(2,1)S(1)}, u32[]{:S(2)}, u32[]{:S(2)}) async-start(bf16[8,32,1792]{2,1,0:T(8,128)(2,1)} %bitcast.332), calls=%async_computation.1 | async-start | bytes 1835008 | tf_op jit(solution)/shard_map/all_to_all | solution.py:175
  188.3 11.3 %collective-permute-start.9 = (bf16[3,256,256]{2,1,0:T(8,128)(2,1)S(1)}, bf16[3,256,256]{2,1,0:T(8,128)(2,1)S(1)}, u32[]{:S(2)}, u32[]{:S(2)}) collective-permute-start(bf16[3,256,256]{2,1,0:T(8,128)(2,1)S(1)} %pad_maximum_fusion.14), channel_id=1, source_target_pairs={{0,2},{1,3},{2,0},{3,1},{4,6},{5,7},{6,4},{7,5},{8,10},{9,11},{10,... | collective-permute-start | bytes 1179656 | tf_op jit(solution)/shard_map/ppermute | solution.py:26
  189.0 20.8 %copy-start.5 = (bf16[3,256,512]{2,1,0:T(8,128)(2,1)}, bf16[3,256,512]{2,1,0:T(8,128)(2,1)S(1)}, u32[]{:S(2)}) copy-start(bf16[3,256,512]{2,1,0:T(8,128)(2,1)S(1)} %pad_maximum_fusion.7.own_ref) | copy-start | bytes 2359300
  189.0 20.8 %collective-permute-start.7 = (bf16[3,256,512]{2,1,0:T(8,128)(2,1)S(1)}, bf16[3,256,512]{2,1,0:T(8,128)(2,1)S(1)}, u32[]{:S(2)}, u32[]{:S(2)}) collective-permute-start(bf16[3,256,512]{2,1,0:T(8,128)(2,1)S(1)} %pad_maximum_fusion.7.own_ref), channel_id=1, source_target_pairs={{0,1},{1,0},{2,3},{3,2},{4,5},{5,4},{6,7},{7,6},{8,9},{9,8},{10,11... | collective-permute-start | bytes 2359304 | tf_op jit(solution)/shard_map/ppermute | solution.py:26
  209.2 9.9 %copy-start.1 = (bf16[8,32,1792]{2,1,0:T(8,128)(2,1)}, bf16[8,32,1792]{2,1,0:T(8,128)(2,1)S(1)}, u32[]{:S(2)}) copy-start(bf16[8,32,1792]{2,1,0:T(8,128)(2,1)S(1)} %all-to-all-done.1) | copy-start | bytes 2752516
  209.2 13.5 %collective-permute-start.10 = (bf16[3,256,256]{2,1,0:T(8,128)(2,1)S(1)}, bf16[3,256,256]{2,1,0:T(8,128)(2,1)}, u32[]{:S(2)}, u32[]{:S(2)}) collective-permute-start(bf16[3,256,256]{2,1,0:T(8,128)(2,1)S(1)} %pad_maximum_fusion.15), channel_id=1, source_target_pairs={{0,2},{1,3},{2,0},{3,1},{4,6},{5,7},{6,4},{7,5},{8,10},{9,11},{10,... | collective-permute-start | bytes 1179656 | tf_op jit(solution)/shard_map/ppermute | solution.py:26
  219.1 26.6 %all-to-all-start.3 = ((bf16[8,32,1792]{2,1,0:T(8,128)(2,1)}), bf16[8,32,1792]{2,1,0:T(8,128)(2,1)S(1)}, u32[]{:S(2)}, u32[]{:S(2)}) async-start(bf16[8,32,1792]{2,1,0:T(8,128)(2,1)} %bitcast.331), calls=%async_computation.3 | async-start | bytes 1835008 | tf_op jit(solution)/shard_map/all_to_all | solution.py:175
  222.7 1.9 collective-permute-start.12
  224.0 4.5 %copy-start.4 = (bf16[3,256,512]{2,1,0:T(8,128)(2,1)}, bf16[3,256,512]{2,1,0:T(8,128)(2,1)S(1)}, u32[]{:S(2)}) copy-start(bf16[3,256,512]{2,1,0:T(8,128)(2,1)S(1)} %pad_maximum_fusion.9.own_ref) | copy-start | bytes 2359300
  224.1 4.5 %collective-permute-start.11 = (bf16[3,256,512]{2,1,0:T(8,128)(2,1)S(1)}, bf16[3,256,512]{2,1,0:T(8,128)(2,1)S(1)}, u32[]{:S(2)}, u32[]{:S(2)}) collective-permute-start(bf16[3,256,512]{2,1,0:T(8,128)(2,1)S(1)} %pad_maximum_fusion.9.own_ref), channel_id=1, source_target_pairs={{0,1},{1,0},{2,3},{3,2},{4,5},{5,4},{6,7},{7,6},{8,9},{9,8},{10,11... | collective-permute-start | bytes 2359304 | tf_op jit(solution)/shard_map/ppermute | solution.py:26
  224.6 3.7 %collective-permute-start.13 = (f32[3,256]{1,0:T(4,128)S(1)}, f32[3,256]{1,0:T(4,128)S(1)}, u32[]{:S(2)}, u32[]{:S(2)}) collective-permute-start(f32[3,256]{1,0:T(4,128)S(1)} %fusion.70), channel_id=1, source_target_pairs={{0,2},{1,3},{2,0},{3,1},{4,6},{5,7},{6,4},{7,5},{8,10},{9,11},{10,... | collective-permute-start | bytes 9224 | tf_op jit(solution)/shard_map/ppermute | solution.py:26
  237.8 11.7 %copy-start.11 = (s32[512,1]{0,1:T(1,128)S(1)}, s32[512,1]{0,1:T(1,128)}, u32[]{:S(2)}) copy-start(s32[512,1]{0,1:T(1,128)} %param.10) | copy-start | bytes 6148
  245.7 3.8 %copy-start = (bf16[8,32,1792]{2,1,0:T(8,128)(2,1)}, bf16[8,32,1792]{2,1,0:T(8,128)(2,1)S(1)}, u32[]{:S(2)}) copy-start(bf16[8,32,1792]{2,1,0:T(8,128)(2,1)S(1)} %all-to-all-done.3) | copy-start | bytes 2752516
  245.7 28.2 %all-to-all-start.5 = ((bf16[8,32,1920]{2,1,0:T(8,128)(2,1)}), bf16[8,32,1920]{2,1,0:T(8,128)(2,1)S(1)}, u32[]{:S(2)}, u32[]{:S(2)}) async-start(bf16[8,32,1920]{2,1,0:T(8,128)(2,1)} %bitcast.85), calls=%async_computation.5 | async-start | bytes 1966080 | tf_op jit(solution)/shard_map/all_to_all | solution.py:175
  275.2 2.6 copy-start.12
  (3 other events, 3.1 us)

commit v2 on v1

v2 whole, which is shorter than its diff:
```python
import functools

import jax
import jax.numpy as jnp
from jax import lax
from jax.experimental import pallas as pl
from jax.experimental.pallas import tpu as pltpu
from jax.sharding import PartitionSpec as P


BALANCE = 1.0
HIGH, LOW = 64, 96
PARTS = (5, 4, 3)
OUT_DIRECT = (False, True, False)
BACK_DIRECT = (False, False, True)
CHUNKS = len(PARTS)


def contract_rows(left, right):
    return lax.dot_general(
        left, right, (((0,), (0,)), ((), ())), preferred_element_type=jnp.float32
    )


def contract_last(left, right):
    return lax.dot_general(
        left, right, (((1,), (1,)), ((), ())), preferred_element_type=jnp.float32
    )


def swap(value, axis, members, bits):
    return lax.ppermute(value, axis, [(i, i ^ bits) for i in range(members)])


def halve(parts, index, members):
    bit = 1
    first = parts
    while bit < members:
        upper = (index & bit) != 0
        half = parts[0].shape[1] // 2
        sent = jnp.stack([jnp.where(upper, v[:, :half], v[:, half:]) for v in parts])
        arrived = swap(sent, "grp", members, bit)
        kept = [jnp.where(upper, v[:, half:], v[:, :half]) for v in parts]
        parts = [k.astype(jnp.float32) + a.astype(jnp.float32) for k, a in zip(kept, arrived)]
        if bit == 1:
            first = parts
        bit *= 2
        if bit < members:
            parts = [v.astype(jnp.bfloat16) for v in parts]
            first = parts if bit == 2 else first
    return parts, first


def double(parts, index, members):
    bit = members // 2
    while bit > 1:
        upper = (index & bit) != 0
        arrived = swap(jnp.stack(parts), "grp", members, bit)
        parts = [
            jnp.concatenate([jnp.where(upper, a, v), jnp.where(upper, v, a)], axis=1)
            for v, a in zip(parts, arrived)
        ]
        bit //= 2
    own = jnp.stack(parts)
    return own, swap(own, "grp", members, bit)


def finish_kernel(experts, reorder, index_ref, place_ref, *refs):
    own_ref, arrived_ref, pair_ref, extra_ref = refs[:4]
    wide_ref, hidden_ref = refs[4:6]
    outs, held_ref = refs[6:-1], refs[-1]
    half = own_ref.shape[2]
    tile = pair_ref.shape[0]

    @pl.when(pl.program_id(0) == 0)
    def _():
        upper = (index_ref[0] & 1) != 0
        for kind in range(3):
            target = hidden_ref if kind == 2 else wide_ref
            base = 2 * half * (kind % 2)

            @pl.when(upper)
            def _():
                target[:, base : base + half] = arrived_ref[kind]
                target[:, base + half : base + 2 * half] = own_ref[kind]

            @pl.when(jnp.logical_not(upper))
            def _():
                target[:, base : base + half] = own_ref[kind]
                target[:, base + half : base + 2 * half] = arrived_ref[kind]

    grad = contract_last(wide_ref[...], pair_ref[...])
    depth = grad.shape[0] // experts
    if not reorder:
        outs[0][...] = grad.astype(jnp.bfloat16)
        return
    held_ref[...] = grad
    for block in range(experts):
        start = pl.multiple_of((block ^ place_ref[0]) * depth, depth)
        rows = pl.ds(start, depth)
        out = outs[block] if len(outs) > 1 else outs[0].at[block * depth : (block + 1) * depth]
        out[:, :tile] = held_ref[rows, :].astype(jnp.bfloat16)
        if out.shape[1] > tile:
            out[:, tile:] = extra_ref[rows, :].astype(jnp.bfloat16)


def tile_of(width, most):
    tiles = [t for t in range(128, most + 1, 128) if width % t == 0]
    return tiles[-1] if tiles else width


def finish(index, place, own, arrived, own_pair, extra, experts, reorder, split):
    kinds, rows, half = own.shape
    width = own_pair.shape[0]
    tile = width if split else tile_of(width, 1024)
    size = rows // experts if split else rows
    lanes = extra.shape[1] if split else 0
    whole = pl.BlockSpec((kinds, rows, half), lambda i, *_: (0, 0, 0))
    results = pl.pallas_call(
        functools.partial(finish_kernel, experts, reorder),
        grid_spec=pltpu.PrefetchScalarGridSpec(
            num_scalar_prefetch=2,
            grid=(width // tile,),
            in_specs=[
                whole,
                whole,
                pl.BlockSpec((tile, 4 * half), lambda i, *_: (i, 0)),
                pl.BlockSpec(extra.shape, lambda i, *_: (0, 0)),
            ],
            out_specs=[
                pl.BlockSpec((rows, 4 * half), lambda i, *_: (0, 0)),
                pl.BlockSpec((rows, 2 * half), lambda i, *_: (0, 0)),
            ]
            + [pl.BlockSpec((size, tile + lanes), lambda i, *_: (0, i))] * (rows // size),
            scratch_shapes=[pltpu.VMEM((rows, tile), jnp.float32)],
        ),
        out_shape=[
            jax.ShapeDtypeStruct((rows, 4 * half), jnp.bfloat16),
            jax.ShapeDtypeStruct((rows, 2 * half), jnp.bfloat16),
        ]
        + [jax.ShapeDtypeStruct((size, width + lanes), jnp.bfloat16)] * (rows // size),
        cost_estimate=pl.CostEstimate(
            flops=8 * rows * width * half, bytes_accessed=8 * width * half, transcendentals=0
        ),
        name="finish",
    )(index.reshape(1), place.reshape(1), own, arrived, own_pair, extra)
    return results[0], results[1], results[2:]


def weights_kernel(*refs):
    scaled, tokens = refs[:CHUNKS], refs[CHUNKS : 2 * CHUNKS]
    pairs, hiddens = refs[2 * CHUNKS : 3 * CHUNKS], refs[3 * CHUNKS : 4 * CHUNKS]
    pair_ref, down_ref, all_scaled, all_tokens, all_pairs, all_hidden = refs[4 * CHUNKS :]

    def gather(target, sources):
        begin = 0
        for source in sources:
            target[begin : begin + source.shape[0]] = source[...]
            begin += source.shape[0]

    @pl.when(pl.program_id(0) == 0)
    def _():
        gather(all_pairs, pairs)
        gather(all_hidden, hiddens)

    gather(all_tokens, tokens)
    gather(all_scaled, scaled)
    pair_ref[...] = contract_rows(all_tokens[...], all_pairs[...]).astype(jnp.bfloat16)
    down_ref[...] = contract_rows(all_hidden[...], all_scaled[...]).astype(jnp.bfloat16)


def weight_grads(arrived, pairs, hiddens, width):
    rows = [v.shape[0] for v in arrived]
    hidden_width = hiddens[0].shape[1]
    tile = tile_of(width, 1024)
    steps = width // tile
    if steps == 1:
        scaled, tokens, shift = (
            [v[:, :width] for v in arrived],
            [v[:, width:] for v in arrived],
            0,
        )
    else:
        scaled, tokens, shift = arrived, arrived, steps
    return pl.pallas_call(
        weights_kernel,
        grid=(steps,),
        in_specs=[pl.BlockSpec((r, tile), lambda i: (0, i)) for r in rows]
        + [pl.BlockSpec((r, tile), lambda i: (0, i + shift)) for r in rows]
        + [pl.BlockSpec((r, 2 * hidden_width), lambda i: (0, 0)) for r in rows]
        + [pl.BlockSpec((r, hidden_width), lambda i: (0, 0)) for r in rows],
        out_specs=[
            pl.BlockSpec((tile, 2 * hidden_width), lambda i: (i, 0)),
            pl.BlockSpec((hidden_width, tile), lambda i: (0, i)),
        ],
        out_shape=[
            jax.ShapeDtypeStruct((width, 2 * hidden_width), jnp.bfloat16),
            jax.ShapeDtypeStruct((hidden_width, width), jnp.bfloat16),
        ],
        scratch_shapes=[
            pltpu.VMEM((sum(rows), tile), jnp.bfloat16),
            pltpu.VMEM((sum(rows), tile), jnp.bfloat16),
            pltpu.VMEM((sum(rows), 2 * hidden_width), jnp.bfloat16),
            pltpu.VMEM((sum(rows), hidden_width), jnp.bfloat16),
        ],
        cost_estimate=pl.CostEstimate(
            flops=6 * sum(rows) * width * hidden_width,
            bytes_accessed=6 * width * hidden_width,
            transcendentals=0,
        ),
        name="weight_grads",
    )(*scaled, *tokens, *pairs, *hiddens)


def activate(gate, up, grad_hidden):
    sigmoid_gate = jax.nn.sigmoid(gate)
    swish = gate * sigmoid_gate
    hidden = (swish * up).astype(jnp.bfloat16)
    inner = jnp.sum(hidden.astype(jnp.float32) * grad_hidden, axis=1)
    grad_gate = (grad_hidden * up * sigmoid_gate * (1.0 + gate * (1.0 - sigmoid_gate))).astype(
        jnp.bfloat16
    )
    grad_up = (grad_hidden * swish).astype(jnp.bfloat16)
    return [grad_gate, grad_up, hidden], inner


def exchange(values, experts):
    sent = values.reshape(experts, values.shape[0] // experts, values.shape[1])
    got = lax.all_to_all(sent, "wide", split_axis=0, concat_axis=0, tiled=True)
    return got.reshape(values.shape)


def join_kernel(*refs):
    out_ref = refs[-1]
    depth = refs[0].shape[0]
    for s, piece in enumerate(refs[:-1]):
        out_ref[s * depth : (s + 1) * depth] = piece[...]


def join(pieces):
    depth, width = pieces[0].shape
    tile = tile_of(width, 1024)
    return pl.pallas_call(
        join_kernel,
        grid=(width // tile,),
        in_specs=[pl.BlockSpec((depth, tile), lambda i: (0, i))] * len(pieces),
        out_specs=pl.BlockSpec((len(pieces) * depth, tile), lambda i: (0, i)),
        out_shape=jax.ShapeDtypeStruct((len(pieces) * depth, width), jnp.bfloat16),
        name="join",
    )(*pieces)


def exchange_direct(pieces, experts):
    got = [None] * experts
    for s in reversed(range(experts)):
        got[s] = pieces[s] if s == 0 else swap(pieces[s], "wide", experts, s)
    return got


def arrange_kernel(experts, begin, depth, direct, live_ref, place_ref, *refs):
    route_ref, probs_ref, upstream_ref, rows_ref = refs[:4]
    outs, slot_ref, select_ref, factor_ref = refs[4:-3], refs[-3], refs[-2], refs[-1]
    count = experts * depth
    step = pl.program_id(0)
    rows_dev = route_ref.shape[1]

    @pl.when(step == 0)
    def _():
        expert = route_ref[...]
        labels = lax.broadcasted_iota(jnp.int32, (experts, rows_dev), 0)
        onehot = (labels == expert).astype(jnp.float32)
        before = lax.broadcasted_iota(jnp.int32, (rows_dev, rows_dev), 0)
        here = lax.broadcasted_iota(jnp.int32, (rows_dev, rows_dev), 1)
        earlier = (before < here).astype(jnp.bfloat16)
        ranks = jnp.dot(
            onehot.astype(jnp.bfloat16), earlier, preferred_element_type=jnp.float32
        )
        slot = jnp.sum(onehot * ranks, axis=0, keepdims=True).astype(jnp.int32)
        slot_ref[...] = slot
        block = expert ^ place_ref[0] if direct else expert
        local = slot - begin
        target = jnp.where((local >= 0) & (local < depth), block * depth + local, -1)
        places = lax.broadcasted_iota(jnp.int32, (count, rows_dev), 0)
        select = (places == target).astype(jnp.float32)
        select_ref[...] = select.astype(jnp.bfloat16)
        inside = lax.broadcasted_iota(jnp.int32, (1, rows_dev), 1) < live_ref[0]
        factor = jnp.where(inside, probs_ref[...], 0.0)
        factor_ref[...] = jnp.sum(select * factor, axis=1, keepdims=True)

    def put(value):
        value = value.astype(jnp.bfloat16)
        if len(outs) == 1:
            outs[0][...] = value
        else:
            for s, out in enumerate(outs):
                out[...] = value[s * depth : (s + 1) * depth]

    half = pl.num_programs(0) // 2

    @pl.when(step < half)
    def _():
        picked = jnp.dot(select_ref[...], upstream_ref[...], preferred_element_type=jnp.float32)
        put(picked * factor_ref[...])

    @pl.when(step >= half)
    def _():
        put(jnp.dot(select_ref[...], rows_ref[...], preferred_element_type=jnp.float32))


def arrange(live, place, route, probs, upstream, rows_in, experts, begin, depth, direct):
    rows_dev, width = upstream.shape
    tile = tile_of(width, 1024)
    half = width // tile
    count = experts * depth
    row = pl.BlockSpec((1, rows_dev), lambda i, *_: (0, 0))
    split = [depth] * experts if direct else [count]
    lanes = -(-width // 128) * 128
    padded = lanes != width
    results = pl.pallas_call(
        functools.partial(arrange_kernel, experts, begin, depth, direct),
        grid_spec=pltpu.PrefetchScalarGridSpec(
            num_scalar_prefetch=2,
            grid=(2 * half,),
            in_specs=[
                row,
                row,
                pl.BlockSpec((rows_dev, tile), lambda i, *_: (0, jnp.minimum(i, half - 1))),
                pl.BlockSpec((rows_dev, tile), lambda i, *_: (0, jnp.maximum(i - half, 0))),
            ],
            out_specs=[
                pl.BlockSpec((None, size, tile), lambda i, *_: (i // half, 0, i % half))
                if padded
                else pl.BlockSpec((size, tile), lambda i, *_: (0, i))
                for size in split
            ]
            + [row],
            scratch_shapes=[
                pltpu.VMEM((count, rows_dev), jnp.bfloat16),
                pltpu.VMEM((count, 1), jnp.float32),
            ],
        ),
        out_shape=[
            jax.ShapeDtypeStruct((2, size, width) if padded else (size, 2 * width), jnp.bfloat16)
            for size in split
        ]
        + [jax.ShapeDtypeStruct((1, rows_dev), jnp.int32)],
        cost_estimate=pl.CostEstimate(
            flops=4 * count * rows_dev * width,
            bytes_accessed=4 * rows_dev * width,
            transcendentals=0,
        ),
        name="arrange",
    )(live, place, route, probs, upstream, rows_in)
    pieces = results[:-1]
    if padded:
        pieces = [jnp.concatenate([v[0], v[1]], axis=1) for v in pieces]
    return pieces, results[-1][0]


def after(value, *others):
    return lax.optimization_barrier((value, *others))[0]


def collect_kernel(experts, per_row, live_ref, place_ref, *refs):
    route_ref, slot_ref, probs_ref, partial_ref = refs[:4]
    pieces, extras = refs[4 : 4 + experts], refs[4 + experts : 4 + 2 * experts]
    rows_ref, prob_ref, select_ref, held_ref, extra_ref = refs[4 + 2 * experts :]
    depth = pieces[0].shape[0]
    count = experts * depth
    rows_dev = route_ref.shape[1]
    begin = per_row * depth - depth

    @pl.when(pl.program_id(0) == 0)
    def _():
        expert, slot = route_ref[...], slot_ref[...]
        block = expert ^ place_ref[0]
        local = slot - begin
        target = jnp.where(local >= 0, block * depth + local, -1)
        places = lax.broadcasted_iota(jnp.int32, (count, rows_dev), 0)
        select_ref[...] = (places == target).astype(jnp.float32).astype(jnp.bfloat16)
        for s in range(experts):
            extra_ref[s * depth : (s + 1) * depth] = extras[s][...].astype(jnp.float32)
        extra = extra_ref[...].astype(jnp.bfloat16)
        source = block * depth + slot // per_row
        chosen = (places == source).astype(jnp.float32).astype(jnp.bfloat16)
        found = contract_rows(extra, chosen)
        lanes = lax.broadcasted_iota(jnp.int32, found.shape, 0)
        inner = jnp.sum(
            jnp.where(lanes == slot % per_row, found, 0.0), axis=0, keepdims=True
        )
        inner = (inner / probs_ref[...]).astype(jnp.bfloat16).astype(jnp.float32)
        heads = (lax.broadcasted_iota(jnp.int32, (count, rows_dev), 0) % depth == 0).astype(
            jnp.float32
        )
        counts = contract_rows(extra, heads.astype(jnp.bfloat16))
        share = jnp.sum(
            jnp.where(lanes == HIGH + expert, 16.0 * counts, 0.0)
            + jnp.where(lanes == LOW + expert, counts, 0.0),
            axis=0,
            keepdims=True,
        )
        inside = lax.broadcasted_iota(jnp.int32, (1, rows_dev), 1) < live_ref[0]
        total = jnp.where(inside, inner + BALANCE * (share / rows_dev), 0.0)
        prob_ref[...] = total.astype(jnp.bfloat16)

    for s in range(experts):
        held_ref[s * depth : (s + 1) * depth] = pieces[s][...].astype(jnp.float32)
    part = contract_rows(select_ref[...], held_ref[...].astype(jnp.bfloat16))
    rows_ref[...] = (part + partial_ref[...].astype(jnp.float32)).astype(jnp.bfloat16)


def collect(live, place, route, slot, probs, partial, pieces, per_row):
    rows_dev, width = partial.shape
    experts = len(pieces)
    depth, _ = pieces[0].shape
    if width % 128 == 0:
        tile, mains, shift = tile_of(width, 1024), pieces, width // 128
    else:
        tile, mains, shift = width, [v[:, :width] for v in pieces], 0
        pieces = [v[:, width:] for v in pieces]
    row = pl.BlockSpec((1, rows_dev), lambda i, *_: (0, 0))
    count = experts * depth
    return pl.pallas_call(
        functools.partial(collect_kernel, experts, per_row),
        grid_spec=pltpu.PrefetchScalarGridSpec(
            num_scalar_prefetch=2,
            grid=(width // tile,),
            in_specs=[row, row, row, pl.BlockSpec((rows_dev, tile), lambda i, *_: (0, i))]
            + [pl.BlockSpec((depth, tile), lambda i, *_: (0, i))] * experts
            + [pl.BlockSpec((depth, 128), lambda i, *_: (0, shift))] * experts,
            out_specs=[pl.BlockSpec((rows_dev, tile), lambda i, *_: (0, i)), row],
            scratch_shapes=[
                pltpu.VMEM((count, rows_dev), jnp.bfloat16),
                pltpu.VMEM((count, tile), jnp.float32),
                pltpu.VMEM((count, 128), jnp.float32),
            ],
        ),
        out_shape=[
            jax.ShapeDtypeStruct((rows_dev, width), jnp.bfloat16),
            jax.ShapeDtypeStruct((1, rows_dev), jnp.bfloat16),
        ],
        name="collect",
    )(live, place, route, slot, probs, partial, *mains, *pieces)


def on_device(rows_in, upstream, probs, route, live, gate_up, down):
    experts = lax.axis_size("wide")
    members = lax.axis_size("grp")
    index = lax.axis_index("grp")
    place = lax.axis_index("wide")
    rows_dev, width = rows_in.shape
    hidden_width = down.shape[1]
    capacity = rows_dev * 3 // (2 * experts)
    depths = [capacity * part // sum(PARTS) // 8 * 8 for part in PARTS]
    depths[0] += capacity - sum(depths)
    begins = [sum(depths[:step]) for step in range(CHUNKS)]
    own_pair = gate_up[0]
    own_down = down[0]
    expert_of = route[:, 0]
    inside = lax.iota(jnp.int32, rows_dev) < live[0]
    live_mask = inside.astype(jnp.float32)
    labels = lax.iota(jnp.int32, experts)
    onehot = (expert_of[:, None] == labels[None, :]).astype(jnp.int32)
    flat = (live, place.reshape(1), route.reshape(1, rows_dev), probs.reshape(1, rows_dev))
    sent = []
    for step in range(CHUNKS):
        pieces, slots = arrange(
            *flat, upstream, rows_in, experts, begins[step], depths[step], OUT_DIRECT[step]
        )
        sent.append(pieces)
        slot = slots if step == 0 else slot

    def selector(step):
        block = expert_of ^ place if BACK_DIRECT[step] else expert_of
        local = slot - begins[step]
        held = (local >= 0) & (local < depths[step])
        target = jnp.where(held, block * depths[step] + local, -1)
        places = lax.iota(jnp.int32, experts * depths[step])
        return (target[None, :] == places[:, None]).astype(jnp.bfloat16)

    def project(block):
        grad_part = contract_last(block[:, :width], own_down).astype(jnp.bfloat16)
        pre_part = jnp.dot(block[:, width:], own_pair, preferred_element_type=jnp.float32)
        pre_part = pre_part.astype(jnp.bfloat16)
        return [pre_part[:, :hidden_width], pre_part[:, hidden_width:], grad_part]

    pairs, hiddens, inners = [], [], []
    arrived, parts, returned = [], [], []
    packed = []

    def receive(step):
        if OUT_DIRECT[step]:
            arrived.append(join(exchange_direct(sent[step], experts)))
        else:
            arrived.append(exchange(sent[step][0], experts))

    def process(step):
        parts.append(project(arrived[step]))
        share, _ = halve(parts[step], index, members)
        values, inner = activate(*share)
        packed.append(values)
        inner = inner.reshape(experts, depths[step])
        inners.append(inner[labels ^ place] if OUT_DIRECT[step] else inner)

    receive(0)
    sent[1] = [after(v, arrived[0]) for v in sent[1]]
    receive(1)
    process(0)
    sent[2] = [after(v, *packed[0]) for v in sent[2]]
    receive(2)
    process(1)
    process(2)
    inner_all = jnp.concatenate(inners, axis=1)
    bit = 1
    while bit < members:
        inner_all = inner_all + swap(inner_all, "grp", members, bit)
        bit *= 2
    local_loads = jnp.sum(onehot * inside.astype(jnp.int32)[:, None], axis=0)
    digits = jnp.concatenate([local_loads // 16, local_loads % 16]).astype(jnp.float32)
    last_rows = experts * depths[-1]
    per_row = capacity // depths[-1]
    blank = jnp.zeros((HIGH - per_row,), jnp.float32)
    gap = jnp.zeros((LOW - HIGH - experts,), jnp.float32)
    rest = jnp.zeros((128 - LOW - experts,), jnp.float32)
    digits = jnp.concatenate([blank, digits[:experts], gap, digits[experts:], rest])
    digits = jnp.broadcast_to(digits[None, :], (last_rows, 128 - per_row))
    extra = jnp.concatenate([inner_all.reshape(last_rows, per_row), digits], axis=1)
    for step in range(CHUNKS):
        own, other = double(packed[step], index, members)
        grad_pair, hidden, outs = finish(
            index,
            place,
            own,
            other,
            own_pair,
            extra if step == CHUNKS - 1 else jnp.zeros((8, 128), jnp.float32),
            experts,
            OUT_DIRECT[step] != BACK_DIRECT[step],
            step == CHUNKS - 1,
        )
        pairs.append(grad_pair)
        hiddens.append(hidden)
        if step == 0:
            outs = [after(outs[0], arrived[-1])]
        if step == 1:
            outs = [after(outs[0], returned[0], *packed[2])]
        if BACK_DIRECT[step]:
            returned.append(exchange_direct(outs, experts))
        else:
            returned.append(exchange(outs[0], experts))

    pair_grad, down_grad = weight_grads(arrived, pairs, hiddens, width)

    partial = None
    for step in range(CHUNKS - 1):
        part = contract_rows(selector(step), returned[step]).astype(jnp.bfloat16)
        partial = part if partial is None else partial + part
    grad_rows, grad_prob = collect(
        flat[0], flat[1], flat[2], slot[None, :], flat[3], partial, returned[-1], per_row
    )
    grad_prob = grad_prob[0]
    return grad_rows, grad_prob, pair_grad[None], down_grad[None]


def solution(mesh):
    return jax.shard_map(
        on_device,
        mesh=mesh,
        in_specs=(
            P("wide", "grp"),
            P("wide", "grp"),
            P("wide"),
            P("wide", None),
            P("wide"),
            P("wide", "grp", None),
            P("wide", None, "grp"),
        ),
        out_specs=(P("wide", "grp"), P("wide"), P("wide", "grp", None), P("wide", None, "grp")),
        check_vma=False,
    )
```

time: 280 us -> 290 us (1.036)
  waiting for transfers between devices: 138 us -> 113 us
  Pallas kernels: 38.9 us -> 58.6 us
  starting transfers between devices: 37.1 us -> 56.8 us
  matrix products: 40.6 us -> 28.4 us
  local copies, waits for them, and re-layouts: 2.51 us -> 8.65 us
    all_to_all x6 -> x4, waiting for transfers between devices: 97.2 us -> 61.1 us  [exchange(): got = lax.all_to_all(sent, 'wide', split_axis=0, concat_axis=0, tiled=True)]
    ppermute x14 -> x28, starting transfers between devices: 10 us -> 32.1 us  [swap(): return lax.ppermute(value, axis, [(i, i ^ bits) for i in range(members)])]
    pallas_call x4 -> x9, Pallas kernels: 38.9 us -> 58.6 us  [the longest x3 20.1 us: finish(): pl.pallas_call(functools.partial(finish_kernel, experts, reorder), grid_s...]
    ppermute x14 -> x28, waiting for transfers between devices: 41.1 us -> 52.3 us  [swap(): return lax.ppermute(value, axis, [(i, i ^ bits) for i in range(members)])]
    dot_general x3 -> x0, matrix products: 9.23 us -> none  [arrange(): jnp.dot(select, both, preferred_element_type=jnp.float32)]
    unnamed x30 -> x94, local copies, waits for them, and re-layouts: 1.81 us -> 6.95 us
    all_to_all x6 -> x4, starting transfers between devices: 27.1 us -> 24.7 us  [exchange(): got = lax.all_to_all(sent, 'wide', split_axis=0, concat_axis=0, tiled=True)]
  transfers between devices with their start and end apart: 20 -> 32, of which waited for: 12 -> 13; matrix products, arithmetic and copies ran while one was open for 14% -> 16% of each run, Pallas kernels for 14% -> 17%
where the time goes in v2:
time: 290 us; the launch traced here: 289 us
  waiting for transfers between devices  113 us (39%)
  Pallas kernels  58.6 us (20%)
  starting transfers between devices  56.8 us (20%)
  matrix products  28.4 us (10%)
  other arithmetic  20.9 us (7%)
  local copies, waits for them, and re-layouts  8.65 us (3%)
    all_to_all x4, waiting for transfers between devices, exchange(): got = lax.all_to_all(sent, 'wide', split_axis=0, concat_axis=0, tiled=True)  61.1 us
    ppermute x28, waiting for transfers between devices, swap(): return lax.ppermute(value, axis, [(i, i ^ bits) for i in range(members)])  52.3 us
    ppermute x28, starting transfers between devices, swap(): return lax.ppermute(value, axis, [(i, i ^ bits) for i in range(members)])  32.1 us
    all_to_all x4, starting transfers between devices, exchange(): got = lax.all_to_all(sent, 'wide', split_axis=0, concat_axis=0, tiled=True)  24.7 us
    pallas_call x3, Pallas kernels, finish(): pl.pallas_call(functools.partial(finish_kernel, experts, reorder), grid_s...  20.1 us
    pallas_call x3, Pallas kernels, arrange(): pl.pallas_call(functools.partial(arrange_kernel, experts, begin, depth, d...  16.5 us
    pallas_call x1, Pallas kernels, weight_grads(): pl.pallas_call(weights_kernel, grid=(steps,), in_specs=[pl.BlockSpec((r,...  15 us
    dot_general x3, matrix products, project(): jnp.dot(block[:, width:], own_pair, preferred_element_type=jnp.float32)  14 us
  transfers between devices with their start and end apart: 32, of which 13 were waited for; matrix products, arithmetic and copies ran while one was open for 16% of the time, Pallas kernels for 17%

profile of v2, /device:TPU:0, one launch (start us, length us, event | category | flops | bytes accessed | tf_op | source)
XLA Modules:
  0.0 289.0 jit_solution(2324453592099611249)
XLA Ops:
  1.3 5.7 %arrange.3 = (bf16[320,3584]{1,0:T(8,128)(2,1)}, s32[1,512]{1,0:T(1,128)}) custom-call(s32[1]{0:T(128)} %copy.11.live_ref, s32[1]{0:T(128)} %bitcast.place_ref, s32[1,512]{1,0:T(1,128)} %bitcast.317, f32[1,512]{1,0:T(1,128)} %bitcast.322, bf16[512,1792]{1,0:T(8,128)(2,1)} %refs_2_.5, bf16[512,1792]{1,0:T(8,128)(2,1)} %refs_3_.5), custom_call_target="tpu_custom_call" | custom-call | flops 1174405120 | bytes 3670016 | tf_op jit(solution)/shard_map/arrange/pallas_call | solution.py:319
  7.0 7.3 %all-to-all-start = ((bf16[8,40,3584]{2,1,0:T(8,128)(2,1)}), bf16[8,40,3584]{2,1,0:T(8,128)(2,1)}, u32[]{:S(2)}, u32[]{:S(2)}) async-start(bf16[8,40,3584]{2,1,0:T(8,128)(2,1)} %bitcast.300), calls=%async_computation | async-start | bytes 4587520 | tf_op jit(solution)/shard_map/all_to_all | solution.py:229
  14.3 5.6 %arrange.5 = (bf16[32,3584]{1,0:T(8,128)(2,1)}, bf16[32,3584]{1,0:T(8,128)(2,1)}, bf16[32,3584]{1,0:T(8,128)(2,1)}, bf16[32,3584]{1,0:T(8,128)(2,1)}, bf16[32,35...) custom-call(s32[1]{0:T(128)} %copy.11.live_ref, ...), custom_call_target="tpu_custom_call" | custom-call | flops 939524096 | bytes 3670016 | tf_op jit(solution)/shard_map/arrange/pallas_call | solution.py:319
  20.0 46.8 %all-to-all-done = bf16[8,40,3584]{2,1,0:T(8,128)(2,1)} async-done(((bf16[8,40,3584]{2,1,0:T(8,128)(2,1)}), bf16[8,40,3584]{2,1,0:T(8,128)(2,1)}, u32[]{:S(2)}, u32[]{:S(2)}) %all-to-all-start) | async-done | bytes 2293792 | tf_op jit(solution)/shard_map/all_to_all | solution.py:229
  71.1 3.0 %collective-permute-start.8 = (bf16[32,3584]{1,0:T(8,128)(2,1)}, bf16[32,3584]{1,0:T(8,128)(2,1)S(1)}, u32[]{:S(2)}, u32[]{:S(2)}) collective-permute-start(bf16[32,3584]{1,0:T(8,128)(2,1)} %get-tuple-element.63), channel_id=1, source_target_pairs={{0,20},{4,16},{8,28},{12,24},{16,4},{20,0},{24,12},{28,8},{1,21},{... | collective-permute-start | bytes 688136 | tf_op jit(solution)/shard_map/ppermute | solution.py:32
  74.1 3.8 %fusion.7 = bf16[320,1024]{1,0:T(8,128)(2,1)S(1)} fusion(bf16[1,1024,1792]{2,1,0:T(8,128)(2,1)} %param.13, bf16[320,3584]{1,0:T(8,128)(2,1)} %bitcast.6.refs_0_.refs_3_), kind=kOutput, calls=%fused_computation.13 | convolution fusion | flops 1174732800 | bytes 5472256 | tf_op jit(solution)/shard_map/dot_general | solution.py:26
  77.9 4.0 %convolution_convert_fusion.2 = bf16[320,2048]{1,0:T(8,128)(2,1)S(1)} fusion(bf16[320,3584]{1,0:T(8,128)(2,1)} %bitcast.6.refs_0_.refs_3_, bf16[1,1792,2048]{2,1,0:T(8,128)(2,1)S(1)} %bitcast.298), kind=kOutput, calls=%fused_computation.10 | convolution fusion | flops 2349465600 | bytes 9797632 | tf_op jit(solution)/shard_map/dot_general | solution.py:483
  87.5 16.9 %collective-permute-done.8.refs_5_ = bf16[32,3584]{1,0:T(8,128)(2,1)S(1)} collective-permute-done((bf16[32,3584]{1,0:T(8,128)(2,1)}, bf16[32,3584]{1,0:T(8,128)(2,1)S(1)}, u32[]{:S(2)}, u32[]{:S(2)}) %collective-permute-start.8) | collective-permute-done | bytes 229408 | tf_op jit(solution)/shard_map/ppermute | solution.py:32
  106.5 3.6 %join.1.refs_1_.refs_4_ = bf16[256,3584]{1,0:T(8,128)(2,1)} custom-call(bf16[32,3584]{1,0:T(8,128)(2,1)} %get-tuple-element.53.refs_0_, bf16[32,3584]{1,0:T(8,128)(2,1)} %copy-done.27, bf16[32,3584]{1,0:T(8,128)(2,1)} %copy-done.28, bf16[32,3584]{1,0:T(8,128)(2,1)} %copy-done.29, bf16[32,3584]{1,0:T(8,128)(2,1)} %copy-done.30, bf16[32,3584]{1,0:T(8,128)(2,1)} %copy-done.31, ...), custom_call_target="tpu_custom_call" | custom-call | tf_op jit(solution)/shard_map/join/pallas_call | solution.py:243
  110.2 3.6 %fusion.10 = bf16[256,1024]{1,0:T(8,128)(2,1)S(1)} fusion(bf16[1,1024,1792]{2,1,0:T(8,128)(2,1)} %param.13, bf16[256,3584]{1,0:T(8,128)(2,1)} %join.1.refs_1_.refs_4_), kind=kOutput, calls=%fused_computation.14 | convolution fusion | flops 939786240 | bytes 5111808 | tf_op jit(solution)/shard_map/dot_general | solution.py:26
  113.8 5.3 %convolution_convert_fusion.3 = bf16[256,2048]{1,0:T(8,128)(2,1)S(1)} fusion(bf16[256,3584]{1,0:T(8,128)(2,1)S(1)} %copy-done.7, bf16[1,1792,2048]{2,1,0:T(8,128)(2,1)} %param.12), kind=kOutput, calls=%fused_computation.11 | convolution fusion | flops 1879572480 | bytes 9306112 | tf_op jit(solution)/shard_map/dot_general | solution.py:483
  124.6 5.2 %arrange.4 = (bf16[192,3584]{1,0:T(8,128)(2,1)}, s32[1,512]{1,0:T(1,128)}) custom-call(s32[1]{0:T(128)} %copy.11.live_ref, s32[1]{0:T(128)} %bitcast.place_ref, s32[1,512]{1,0:T(1,128)} %bitcast.319, f32[1,512]{1,0:T(1,128)} %bitcast.324, bf16[512,1792]{1,0:T(8,128)(2,1)} %refs_2_.5, bf16[512,1792]{1,0:T(8,128)(2,1)} %refs_3_.5), custom_call_target="tpu_custom_call" | custom-call | flops 704643072 | bytes 3670016 | tf_op jit(solution)/shard_map/arrange/pallas_call | solution.py:319
  131.8 4.0 %collective-permute-done.1 = bf16[3,320,256]{2,1,0:T(8,128)(2,1)} collective-permute-done((bf16[3,320,256]{2,1,0:T(8,128)(2,1)}, bf16[3,320,256]{2,1,0:T(8,128)(2,1)}, u32[]{:S(2)}, u32[]{:S(2)}) %collective-permute-start.1) | collective-permute-done | bytes 491552 | tf_op jit(solution)/shard_map/ppermute | solution.py:32
  138.6 10.3 %all-to-all-start.1 = ((bf16[8,24,3584]{2,1,0:T(8,128)(2,1)}), bf16[8,24,3584]{2,1,0:T(8,128)(2,1)S(1)}, u32[]{:S(2)}, u32[]{:S(2)}) async-start(bf16[8,24,3584]{2,1,0:T(8,128)(2,1)} %bitcast.308), calls=%async_computation.1 | async-start | bytes 2752512 | tf_op jit(solution)/shard_map/all_to_all | solution.py:229
  152.3 8.8 %collective-permute-done.12 = bf16[3,256,256]{2,1,0:T(8,128)(2,1)S(1)} collective-permute-done((bf16[3,256,256]{2,1,0:T(8,128)(2,1)S(1)}, bf16[3,256,256]{2,1,0:T(8,128)(2,1)S(1)}, u32[]{:S(2)}, u32[]{:S(2)}) %collective-permute-start.12) | collective-permute-done | bytes 393248 | tf_op jit(solution)/shard_map/ppermute | solution.py:32
  163.9 7.6 %collective-permute-done.2 = bf16[3,320,256]{2,1,0:T(8,128)(2,1)S(1)} collective-permute-done((bf16[3,320,256]{2,1,0:T(8,128)(2,1)S(1)}, bf16[3,320,256]{2,1,0:T(8,128)(2,1)S(1)}, u32[]{:S(2)}, u32[]{:S(2)}) %collective-permute-start.2) | collective-permute-done | bytes 491552 | tf_op jit(solution)/shard_map/ppermute | solution.py:32
  172.0 8.5 %all-to-all-done.1 = bf16[8,24,3584]{2,1,0:T(8,128)(2,1)S(1)} async-done(((bf16[8,24,3584]{2,1,0:T(8,128)(2,1)}), bf16[8,24,3584]{2,1,0:T(8,128)(2,1)S(1)}, u32[]{:S(2)}, u32[]{:S(2)}) %all-to-all-start.1) | async-done | bytes 1376288 | tf_op jit(solution)/shard_map/all_to_all | solution.py:229
  180.5 3.9 %fusion.13 = bf16[192,1024]{1,0:T(8,128)(2,1)S(1)} fusion(bf16[1,1024,1792]{2,1,0:T(8,128)(2,1)} %param.13, bf16[192,3584]{1,0:T(8,128)(2,1)S(1)} %bitcast.304), kind=kOutput, calls=%fused_computation.15 | convolution fusion | flops 704839680 | bytes 4751360 | tf_op jit(solution)/shard_map/dot_general | solution.py:26
  184.4 4.7 %convolution_convert_fusion.4 = bf16[192,2048]{1,0:T(8,128)(2,1)S(1)} fusion(bf16[192,3584]{1,0:T(8,128)(2,1)S(1)} %bitcast.305, bf16[1,1792,2048]{2,1,0:T(8,128)(2,1)} %param.12), kind=kOutput, calls=%fused_computation.12 | convolution fusion | flops 1409679360 | bytes 8814592 | tf_op jit(solution)/shard_map/dot_general | solution.py:483
  193.9 6.7 %finish.3 = (bf16[320,2048]{1,0:T(8,128)(2,1)}, bf16[320,1024]{1,0:T(8,128)(2,1)}, bf16[320,1792]{1,0:T(8,128)(2,1)}) custom-call(s32[1]{0:T(128)} %bitcast.4.index_ref, s32[1]{0:T(128)} %bitcast.place_ref, bf16[3,320,512]{2,1,0:T(8,128)(2,1)} %copy-done.2, bf16[3,320,512]{2,1,0:T(8,128)(2,1)} %collective-permute-done.3.refs_1_, ...), custom_call_target="tpu_custom_call" | custom-call | flops 2348810240 | bytes 7340032 | tf_op jit(solution)/shard_map/finish/pallas_call | solution.py:119
  200.6 3.6 %all-to-all-start.2 = ((bf16[8,40,1792]{2,1,0:T(8,128)(2,1)}), bf16[8,40,1792]{2,1,0:T(8,128)(2,1)S(1)}, u32[]{:S(2)}, u32[]{:S(2)}) async-start(bf16[8,40,1792]{2,1,0:T(8,128)(2,1)} %bitcast.313), calls=%async_computation.2 | async-start | bytes 2293760 | tf_op jit(solution)/shard_map/all_to_all | solution.py:229
  207.8 7.4 %collective-permute-done.16 = bf16[3,192,256]{2,1,0:T(8,128)(2,1)S(1)} collective-permute-done((bf16[3,192,256]{2,1,0:T(8,128)(2,1)S(1)}, bf16[3,192,256]{2,1,0:T(8,128)(2,1)S(1)}, u32[]{:S(2)}, u32[]{:S(2)}) %collective-permute-start.16) | collective-permute-done | bytes 294944 | tf_op jit(solution)/shard_map/ppermute | solution.py:32
  219.7 6.1 %finish.4 = (bf16[256,2048]{1,0:T(8,128)(2,1)}, bf16[256,1024]{1,0:T(8,128)(2,1)}, bf16[256,1792]{1,0:T(8,128)(2,1)}) custom-call(s32[1]{0:T(128)} %bitcast.4.index_ref, s32[1]{0:T(128)} %bitcast.place_ref, bf16[3,256,512]{2,1,0:T(8,128)(2,1)} %copy-done.3, bf16[3,256,512]{2,1,0:T(8,128)(2,1)} %copy-done.17, bf16[1792,2048]{1,0:T(8,128)(2,1)} %bitcast.295, ...), custom_call_target="tpu_custom_call" | custom-call | flops 1879048192 | bytes 7340032 | tf_op jit(solution)/shard_map/finish/pallas_call | solution.py:119
  227.2 5.8 %all-to-all-done.2 = bf16[8,40,1792]{2,1,0:T(8,128)(2,1)S(1)} async-done(((bf16[8,40,1792]{2,1,0:T(8,128)(2,1)}), bf16[8,40,1792]{2,1,0:T(8,128)(2,1)S(1)}, u32[]{:S(2)}, u32[]{:S(2)}) %all-to-all-start.2) | async-done | bytes 1146912 | tf_op jit(solution)/shard_map/all_to_all | solution.py:229
  232.9 3.6 %all-to-all-start.3 = ((bf16[8,32,1792]{2,1,0:T(8,128)(2,1)}), bf16[8,32,1792]{2,1,0:T(8,128)(2,1)S(1)}, u32[]{:S(2)}, u32[]{:S(2)}) async-start(bf16[8,32,1792]{2,1,0:T(8,128)(2,1)} %bitcast.68), calls=%async_computation.3 | async-start | bytes 1835008 | tf_op jit(solution)/shard_map/all_to_all | solution.py:229
  242.0 7.2 %finish.5 = (bf16[192,2048]{1,0:T(8,128)(2,1)}, bf16[192,1024]{1,0:T(8,128)(2,1)}, bf16[24,1920]{1,0:T(8,128)(2,1)}, bf16[24,1920]{1,0:T(8,128)(2,1)}, bf16[24,1...) custom-call(s32[1]{0:T(128)} %bitcast.4.index_ref, ...), custom_call_target="tpu_custom_call" | custom-call | flops 1409286144 | bytes 7340032 | tf_op jit(solution)/shard_map/finish/pallas_call | solution.py:119
  252.8 2.9 collective-permute-start.24
  257.1 15.0 %weight_grads.1 = (bf16[1792,2048]{1,0:T(8,128)(2,1)}, bf16[1024,1792]{1,0:T(8,128)(2,1)}) custom-call(bf16[320,3584]{1,0:T(8,128)(2,1)} %bitcast.6.refs_0_.refs_3_, bf16[256,3584]{1,0:T(8,128)(2,1)} %join.1.refs_1_.refs_4_, bf16[192,3584]{1,0:T(8,128)(2,1)} %bitcast.306, bf16[320,3584]{1,0:T(8,128)(2,1)} %bitcast.6.refs_0_.refs_3_, ...), custom_call_target="tpu_custom_call" | custom-call | flops 8455716864 | bytes 11010048 | tf_op jit(solution)/shard_map/weight_grads/pallas_call | solution.py:185
  273.0 3.3 %collective-permute-start.26 = (bf16[24,1920]{1,0:T(8,128)(2,1)S(1)}, bf16[24,1920]{1,0:T(8,128)(2,1)S(1)}, u32[]{:S(2)}, u32[]{:S(2)}) collective-permute-start(bf16[24,1920]{1,0:T(8,128)(2,1)S(1)} %copy-done.42), channel_id=1, source_target_pairs={{0,24},{4,28},{8,16},{12,20},{16,8},{20,12},{24,0},{28,4},{1,25},{... | collective-permute-start | bytes 276488 | tf_op jit(solution)/shard_map/ppermute | solution.py:32
  276.4 2.4 fusion.6.refs_3_
  280.1 3.5 %collective-permute-done.27.refs_11_.refs_19_ = bf16[24,1920]{1,0:T(8,128)(2,1)S(1)} collective-permute-done((bf16[24,1920]{1,0:T(8,128)(2,1)S(1)}, bf16[24,1920]{1,0:T(8,128)(2,1)S(1)}, u32[]{:S(2)}, u32[]{:S(2)}) %collective-permute-start.27) | collective-permute-done | bytes 92192 | tf_op jit(solution)/shard_map/ppermute | solution.py:32
  284.2 3.5 %collect.1 = (bf16[512,1792]{1,0:T(8,128)(2,1)}, bf16[1,512]{1,0:T(2,128)(2,1)}) custom-call(s32[1]{0:T(128)} %copy.11.live_ref, s32[1]{0:T(128)} %bitcast.place_ref, s32[1,512]{1,0:T(1,128)} %bitcast.320, s32[1,512]{1,0:T(1,128)} %get-tuple-element.46.refs_1_, f32[1,512]{1,0:T(1,128)} %bitcast.325, bf16[512,1792]{1,0:T(8,128)(2,1)} %fusion.6.refs_3_, ...), custom_call_target="tpu_custom_call" | custom-call | tf_op jit(solution)/shard_map/collect/pallas_call | solution.py:423
  (213 shorter events, 57.4 us)
Async XLA Ops:
  7.0 59.8 %all-to-all-start = ((bf16[8,40,3584]{2,1,0:T(8,128)(2,1)}), bf16[8,40,3584]{2,1,0:T(8,128)(2,1)}, u32[]{:S(2)}, u32[]{:S(2)}) async-start(bf16[8,40,3584]{2,1,0:T(8,128)(2,1)} %bitcast.300), calls=%async_computation | async-start | bytes 4587520 | tf_op jit(solution)/shard_map/all_to_all | solution.py:229
  66.8 15.3 %collective-permute-start.4 = (bf16[32,3584]{1,0:T(8,128)(2,1)}, bf16[32,3584]{1,0:T(8,128)(2,1)S(1)}, u32[]{:S(2)}, u32[]{:S(2)}) collective-permute-start(bf16[32,3584]{1,0:T(8,128)(2,1)} %get-tuple-element.55), channel_id=1, source_target_pairs={{0,4},{4,0},{8,12},{12,8},{16,20},{20,16},{24,28},{28,24},{1,5},{5... | collective-permute-start | bytes 688136 | tf_op jit(solution)/shard_map/ppermute | solution.py:32
  68.3 17.1 %collective-permute-start.5 = (bf16[32,3584]{1,0:T(8,128)(2,1)}, bf16[32,3584]{1,0:T(8,128)(2,1)S(1)}, u32[]{:S(2)}, u32[]{:S(2)}) collective-permute-start(bf16[32,3584]{1,0:T(8,128)(2,1)} %get-tuple-element.57), channel_id=1, source_target_pairs={{0,8},{4,12},{8,0},{12,4},{16,24},{20,28},{24,16},{28,20},{1,9},{5... | collective-permute-start | bytes 688136 | tf_op jit(solution)/shard_map/ppermute | solution.py:32
  68.3 19.2 %collective-permute-start.6 = (bf16[32,3584]{1,0:T(8,128)(2,1)}, bf16[32,3584]{1,0:T(8,128)(2,1)S(1)}, u32[]{:S(2)}, u32[]{:S(2)}) collective-permute-start(bf16[32,3584]{1,0:T(8,128)(2,1)} %get-tuple-element.59), channel_id=1, source_target_pairs={{0,12},{4,8},{8,4},{12,0},{16,28},{20,24},{24,20},{28,16},{1,13},{... | collective-permute-start | bytes 688136 | tf_op jit(solution)/shard_map/ppermute | solution.py:32
  70.3 17.2 %collective-permute-start.7 = (bf16[32,3584]{1,0:T(8,128)(2,1)}, bf16[32,3584]{1,0:T(8,128)(2,1)S(1)}, u32[]{:S(2)}, u32[]{:S(2)}) collective-permute-start(bf16[32,3584]{1,0:T(8,128)(2,1)} %get-tuple-element.61), channel_id=1, source_target_pairs={{0,16},{4,20},{8,24},{12,28},{16,0},{20,4},{24,8},{28,12},{1,17},{... | collective-permute-start | bytes 688136 | tf_op jit(solution)/shard_map/ppermute | solution.py:32
  71.1 33.4 %collective-permute-start.8 = (bf16[32,3584]{1,0:T(8,128)(2,1)}, bf16[32,3584]{1,0:T(8,128)(2,1)S(1)}, u32[]{:S(2)}, u32[]{:S(2)}) collective-permute-start(bf16[32,3584]{1,0:T(8,128)(2,1)} %get-tuple-element.63), channel_id=1, source_target_pairs={{0,20},{4,16},{8,28},{12,24},{16,4},{20,0},{24,12},{28,8},{1,21},{... | collective-permute-start | bytes 688136 | tf_op jit(solution)/shard_map/ppermute | solution.py:32
  83.2 21.3 %collective-permute-start.9 = (bf16[32,3584]{1,0:T(8,128)(2,1)S(1)}, bf16[32,3584]{1,0:T(8,128)(2,1)S(1)}, u32[]{:S(2)}, u32[]{:S(2)}) collective-permute-start(bf16[32,3584]{1,0:T(8,128)(2,1)S(1)} %copy-done.40), channel_id=1, source_target_pairs={{0,24},{4,28},{8,16},{12,20},{16,8},{20,12},{24,0},{28,4},{1,25},{... | collective-permute-start | bytes 688136 | tf_op jit(solution)/shard_map/ppermute | solution.py:32
  85.4 19.8 %collective-permute-start.10 = (bf16[32,3584]{1,0:T(8,128)(2,1)S(1)}, bf16[32,3584]{1,0:T(8,128)(2,1)S(1)}, u32[]{:S(2)}, u32[]{:S(2)}) collective-permute-start(bf16[32,3584]{1,0:T(8,128)(2,1)S(1)} %copy-done.39), channel_id=1, source_target_pairs={{0,28},{4,24},{8,20},{12,16},{16,12},{20,8},{24,4},{28,0},{1,29},{... | collective-permute-start | bytes 688136 | tf_op jit(solution)/shard_map/ppermute | solution.py:32
  87.5 31.8 %collective-permute-start = (bf16[3,320,512]{2,1,0:T(8,128)(2,1)S(1)}, bf16[3,320,512]{2,1,0:T(8,128)(2,1)}, u32[]{:S(2)}, u32[]{:S(2)}) collective-permute-start(bf16[3,320,512]{2,1,0:T(8,128)(2,1)S(1)} %pad_maximum_fusion), channel_id=1, source_target_pairs={{0,1},{1,0},{2,3},{3,2},{4,5},{5,4},{6,7},{7,6},{8,9},{9,8},{10,11... | collective-permute-start | bytes 2949128 | tf_op jit(solution)/shard_map/ppermute | solution.py:32
  119.3 11.1 %collective-permute-start.11 = (bf16[3,256,512]{2,1,0:T(8,128)(2,1)S(1)}, bf16[3,256,512]{2,1,0:T(8,128)(2,1)}, u32[]{:S(2)}, u32[]{:S(2)}) collective-permute-start(bf16[3,256,512]{2,1,0:T(8,128)(2,1)S(1)} %pad_maximum_fusion.2), channel_id=1, source_target_pairs={{0,1},{1,0},{2,3},{3,2},{4,5},{5,4},{6,7},{7,6},{8,9},{9,8},{10,11... | collective-permute-start | bytes 2359304 | tf_op jit(solution)/shard_map/ppermute | solution.py:32
  123.1 12.7 %collective-permute-start.1 = (bf16[3,320,256]{2,1,0:T(8,128)(2,1)}, bf16[3,320,256]{2,1,0:T(8,128)(2,1)}, u32[]{:S(2)}, u32[]{:S(2)}) collective-permute-start(bf16[3,320,256]{2,1,0:T(8,128)(2,1)} %pad_maximum_fusion.6), channel_id=1, source_target_pairs={{0,2},{1,3},{2,0},{3,1},{4,6},{5,7},{6,4},{7,5},{8,10},{9,11},{10,... | collective-permute-start | bytes 1474568 | tf_op jit(solution)/shard_map/ppermute | solution.py:32
  138.6 41.9 %all-to-all-start.1 = ((bf16[8,24,3584]{2,1,0:T(8,128)(2,1)}), bf16[8,24,3584]{2,1,0:T(8,128)(2,1)S(1)}, u32[]{:S(2)}, u32[]{:S(2)}) async-start(bf16[8,24,3584]{2,1,0:T(8,128)(2,1)} %bitcast.308), calls=%async_computation.1 | async-start | bytes 2752512 | tf_op jit(solution)/shard_map/all_to_all | solution.py:229
  149.0 12.1 %collective-permute-start.12 = (bf16[3,256,256]{2,1,0:T(8,128)(2,1)S(1)}, bf16[3,256,256]{2,1,0:T(8,128)(2,1)S(1)}, u32[]{:S(2)}, u32[]{:S(2)}) collective-permute-start(bf16[3,256,256]{2,1,0:T(8,128)(2,1)S(1)} %pad_maximum_fusion.8), channel_id=1, source_target_pairs={{0,2},{1,3},{2,0},{3,1},{4,6},{5,7},{6,4},{7,5},{8,10},{9,11},{10,... | collective-permute-start | bytes 1179656 | tf_op jit(solution)/shard_map/ppermute | solution.py:32
  151.7 19.9 %collective-permute-start.2 = (bf16[3,320,256]{2,1,0:T(8,128)(2,1)S(1)}, bf16[3,320,256]{2,1,0:T(8,128)(2,1)S(1)}, u32[]{:S(2)}, u32[]{:S(2)}) collective-permute-start(bf16[3,320,256]{2,1,0:T(8,128)(2,1)S(1)} %pad_maximum_fusion.7), channel_id=1, source_target_pairs={{0,2},{1,3},{2,0},{3,1},{4,6},{5,7},{6,4},{7,5},{8,10},{9,11},{10,... | collective-permute-start | bytes 1474568 | tf_op jit(solution)/shard_map/ppermute | solution.py:32
  162.4 27.6 %collective-permute-start.13 = (bf16[3,256,256]{2,1,0:T(8,128)(2,1)}, bf16[3,256,256]{2,1,0:T(8,128)(2,1)}, u32[]{:S(2)}, u32[]{:S(2)}) collective-permute-start(bf16[3,256,256]{2,1,0:T(8,128)(2,1)} %pad_maximum_fusion.9), channel_id=1, source_target_pairs={{0,2},{1,3},{2,0},{3,1},{4,6},{5,7},{6,4},{7,5},{8,10},{9,11},{10,... | collective-permute-start | bytes 1179656 | tf_op jit(solution)/shard_map/ppermute | solution.py:32
  171.9 21.4 %collective-permute-start.3 = (bf16[3,320,512]{2,1,0:T(8,128)(2,1)S(1)}, bf16[3,320,512]{2,1,0:T(8,128)(2,1)}, u32[]{:S(2)}, u32[]{:S(2)}) collective-permute-start(bf16[3,320,512]{2,1,0:T(8,128)(2,1)S(1)} %pad_maximum_fusion.1.refs_0_), channel_id=1, source_target_pairs={{0,1},{1,0},{2,3},{3,2},{4,5},{5,4},{6,7},{7,6},{8,9},{9,8},{10,11... | collective-permute-start | bytes 2949128 | tf_op jit(solution)/shard_map/ppermute | solution.py:32
  190.1 14.2 %collective-permute-start.15 = (bf16[3,192,512]{2,1,0:T(8,128)(2,1)}, bf16[3,192,512]{2,1,0:T(8,128)(2,1)}, u32[]{:S(2)}, u32[]{:S(2)}) collective-permute-start(bf16[3,192,512]{2,1,0:T(8,128)(2,1)} %pad_maximum_fusion.4), channel_id=1, source_target_pairs={{0,1},{1,0},{2,3},{3,2},{4,5},{5,4},{6,7},{7,6},{8,9},{9,8},{10,11... | collective-permute-start | bytes 1769480 | tf_op jit(solution)/shard_map/ppermute | solution.py:32
  200.6 32.3 %all-to-all-start.2 = ((bf16[8,40,1792]{2,1,0:T(8,128)(2,1)}), bf16[8,40,1792]{2,1,0:T(8,128)(2,1)S(1)}, u32[]{:S(2)}, u32[]{:S(2)}) async-start(bf16[8,40,1792]{2,1,0:T(8,128)(2,1)} %bitcast.313), calls=%async_computation.2 | async-start | bytes 2293760 | tf_op jit(solution)/shard_map/all_to_all | solution.py:229
  205.8 9.5 %collective-permute-start.16 = (bf16[3,192,256]{2,1,0:T(8,128)(2,1)S(1)}, bf16[3,192,256]{2,1,0:T(8,128)(2,1)S(1)}, u32[]{:S(2)}, u32[]{:S(2)}) collective-permute-start(bf16[3,192,256]{2,1,0:T(8,128)(2,1)S(1)} %pad_maximum_fusion.10), channel_id=1, source_target_pairs={{0,2},{1,3},{2,0},{3,1},{4,6},{5,7},{6,4},{7,5},{8,10},{9,11},{10,... | collective-permute-start | bytes 884744 | tf_op jit(solution)/shard_map/ppermute | solution.py:32
  207.5 11.2 %collective-permute-start.14 = (bf16[3,256,512]{2,1,0:T(8,128)(2,1)S(1)}, bf16[3,256,512]{2,1,0:T(8,128)(2,1)S(1)}, u32[]{:S(2)}, u32[]{:S(2)}) collective-permute-start(bf16[3,256,512]{2,1,0:T(8,128)(2,1)S(1)} %pad_maximum_fusion.3.refs_0_), channel_id=1, source_target_pairs={{0,1},{1,0},{2,3},{3,2},{4,5},{5,4},{6,7},{7,6},{8,9},{9,8},{10,11... | collective-permute-start | bytes 2359304 | tf_op jit(solution)/shard_map/ppermute | solution.py:32
  216.4 9.6 %collective-permute-start.17 = (bf16[3,192,256]{2,1,0:T(8,128)(2,1)}, bf16[3,192,256]{2,1,0:T(8,128)(2,1)}, u32[]{:S(2)}, u32[]{:S(2)}) collective-permute-start(bf16[3,192,256]{2,1,0:T(8,128)(2,1)} %pad_maximum_fusion.11), channel_id=1, source_target_pairs={{0,2},{1,3},{2,0},{3,1},{4,6},{5,7},{6,4},{7,5},{8,10},{9,11},{10,... | collective-permute-start | bytes 884744 | tf_op jit(solution)/shard_map/ppermute | solution.py:32
  226.0 10.7 %collective-permute-start.19 = (f32[8,96]{1,0:T(8,128)S(1)}, f32[8,96]{1,0:T(8,128)S(1)}, u32[]{:S(2)}, u32[]{:S(2)}) collective-permute-start(f32[8,96]{1,0:T(8,128)S(1)} %pad_maximum_fusion.13), channel_id=1, source_target_pairs={{0,1},{1,0},{2,3},{3,2},{4,5},{5,4},{6,7},{7,6},{8,9},{9,8},{10,11... | collective-permute-start | bytes 9224 | tf_op jit(solution)/shard_map/ppermute | solution.py:32
  232.9 39.2 %all-to-all-start.3 = ((bf16[8,32,1792]{2,1,0:T(8,128)(2,1)}), bf16[8,32,1792]{2,1,0:T(8,128)(2,1)S(1)}, u32[]{:S(2)}, u32[]{:S(2)}) async-start(bf16[8,32,1792]{2,1,0:T(8,128)(2,1)} %bitcast.68), calls=%async_computation.3 | async-start | bytes 1835008 | tf_op jit(solution)/shard_map/all_to_all | solution.py:229
  236.6 4.6 %collective-permute-start.18 = (bf16[3,192,512]{2,1,0:T(8,128)(2,1)S(1)}, bf16[3,192,512]{2,1,0:T(8,128)(2,1)S(1)}, u32[]{:S(2)}, u32[]{:S(2)}) collective-permute-start(bf16[3,192,512]{2,1,0:T(8,128)(2,1)S(1)} %pad_maximum_fusion.5.refs_0_), channel_id=1, source_target_pairs={{0,1},{1,0},{2,3},{3,2},{4,5},{5,4},{6,7},{7,6},{8,9},{9,8},{10,11... | collective-permute-start | bytes 1769480 | tf_op jit(solution)/shard_map/ppermute | solution.py:32
  236.8 3.6 %collective-permute-start.20 = (f32[8,96]{1,0:T(8,128)S(1)}, f32[8,96]{1,0:T(8,128)S(1)}, u32[]{:S(2)}, u32[]{:S(2)}) collective-permute-start(f32[8,96]{1,0:T(8,128)S(1)} %fusion.44), channel_id=1, source_target_pairs={{0,2},{1,3},{2,0},{3,1},{4,6},{5,7},{6,4},{7,5},{8,10},{9,11},{10,... | collective-permute-start | bytes 9224 | tf_op jit(solution)/shard_map/ppermute | solution.py:32
  249.2 23.7 %collective-permute-start.21 = (bf16[24,1920]{1,0:T(8,128)(2,1)}, bf16[24,1920]{1,0:T(8,128)(2,1)S(1)}, u32[]{:S(2)}, u32[]{:S(2)}) collective-permute-start(bf16[24,1920]{1,0:T(8,128)(2,1)} %get-tuple-element.71), channel_id=1, source_target_pairs={{0,4},{4,0},{8,12},{12,8},{16,20},{20,16},{24,28},{28,24},{1,5},{5... | collective-permute-start | bytes 276488 | tf_op jit(solution)/shard_map/ppermute | solution.py:32
  251.2 25.0 %collective-permute-start.22 = (bf16[24,1920]{1,0:T(8,128)(2,1)}, bf16[24,1920]{1,0:T(8,128)(2,1)S(1)}, u32[]{:S(2)}, u32[]{:S(2)}) collective-permute-start(bf16[24,1920]{1,0:T(8,128)(2,1)} %get-tuple-element.72), channel_id=1, source_target_pairs={{0,8},{4,12},{8,0},{12,4},{16,24},{20,28},{24,16},{28,20},{1,9},{5... | collective-permute-start | bytes 276488 | tf_op jit(solution)/shard_map/ppermute | solution.py:32
  252.7 26.1 %collective-permute-start.23 = (bf16[24,1920]{1,0:T(8,128)(2,1)}, bf16[24,1920]{1,0:T(8,128)(2,1)S(1)}, u32[]{:S(2)}, u32[]{:S(2)}) collective-permute-start(bf16[24,1920]{1,0:T(8,128)(2,1)} %get-tuple-element.73), channel_id=1, source_target_pairs={{0,12},{4,8},{8,4},{12,0},{16,28},{20,24},{24,20},{28,16},{1,13},{... | collective-permute-start | bytes 276488 | tf_op jit(solution)/shard_map/ppermute | solution.py:32
  252.8 26.1 %collective-permute-start.24 = (bf16[24,1920]{1,0:T(8,128)(2,1)}, bf16[24,1920]{1,0:T(8,128)(2,1)S(1)}, u32[]{:S(2)}, u32[]{:S(2)}) collective-permute-start(bf16[24,1920]{1,0:T(8,128)(2,1)} %get-tuple-element.74), channel_id=1, source_target_pairs={{0,16},{4,20},{8,24},{12,28},{16,0},{20,4},{24,8},{28,12},{1,17},{... | collective-permute-start | bytes 276488 | tf_op jit(solution)/shard_map/ppermute | solution.py:32
  255.6 23.2 %collective-permute-start.25 = (bf16[24,1920]{1,0:T(8,128)(2,1)}, bf16[24,1920]{1,0:T(8,128)(2,1)S(1)}, u32[]{:S(2)}, u32[]{:S(2)}) collective-permute-start(bf16[24,1920]{1,0:T(8,128)(2,1)} %get-tuple-element.75), channel_id=1, source_target_pairs={{0,20},{4,16},{8,28},{12,24},{16,4},{20,0},{24,12},{28,8},{1,21},{... | collective-permute-start | bytes 276488 | tf_op jit(solution)/shard_map/ppermute | solution.py:32
  273.0 7.1 %collective-permute-start.26 = (bf16[24,1920]{1,0:T(8,128)(2,1)S(1)}, bf16[24,1920]{1,0:T(8,128)(2,1)S(1)}, u32[]{:S(2)}, u32[]{:S(2)}) collective-permute-start(bf16[24,1920]{1,0:T(8,128)(2,1)S(1)} %copy-done.42), channel_id=1, source_target_pairs={{0,24},{4,28},{8,16},{12,20},{16,8},{20,12},{24,0},{28,4},{1,25},{... | collective-permute-start | bytes 276488 | tf_op jit(solution)/shard_map/ppermute | solution.py:32
  276.3 7.3 %collective-permute-start.27 = (bf16[24,1920]{1,0:T(8,128)(2,1)S(1)}, bf16[24,1920]{1,0:T(8,128)(2,1)S(1)}, u32[]{:S(2)}, u32[]{:S(2)}) collective-permute-start(bf16[24,1920]{1,0:T(8,128)(2,1)S(1)} %copy-done.41), channel_id=1, source_target_pairs={{0,28},{4,24},{8,20},{12,16},{16,12},{20,8},{24,4},{28,0},{1,29},{... | collective-permute-start | bytes 276488 | tf_op jit(solution)/shard_map/ppermute | solution.py:32
  (47 other events, 309.9 us)
